TPU v7x, 128 devices: a whole 4x4x4 slice. The times are simulated.
128 devices in a mesh: grp: 4 (over z_lo, core), tile: 32 (over x, y, z_hi).
Axes of the slice: x: 4, y: 4, z: 4 (z_hi: 2, z_lo: 2; z = z_hi * 2 + z_lo), core: 2. Of those that a mesh axis runs over, the one named last changes fastest.
Arguments:
- start_velocity: float32 [2, 128, 16384], P(None, 'grp', 'tile'), may hold values from -6 to 6
- driving_stress: float32 [2, 128, 16384], P(None, 'grp', 'tile'), may hold values from -6 to 6
- viscosity: float32 [2, 128, 16384], P(None, 'grp', 'tile'), may hold values from 0.3 to 3
- friction: float32 [128, 16384], P('grp', 'tile'), may hold values from 0.02 to 0.5
- cell_element: int32 [128, 16384], P('grp', 'tile'), may hold values from 0 to 16383, as said below
- observed: float32 [65536, 256], P(('grp', 'tile')), may hold values from -6 to 6
- look: float32 [2, 65536, 256], P(None, ('grp', 'tile')), may hold values from -3 to 3
- row_owner: int32 [65536, 1], P(('grp', 'tile')), may hold values from 0 to 127; in each aligned block of 512 rows (0 to 511, 512 to 1023, ...) at most 8 rows name the same one
- row_cell: int32 [65536], P(('grp', 'tile')), may hold values from 0 to 16383
Outputs:
- stress_adjoint: float32 [2, 128, 16384], P(None, 'grp', 'tile')
- friction_adjoint: float32 [16384], P(('grp', 'tile'))
Inputs may be any that keep to these rules, and one draw needn't show every extreme that they name: `row_owner`: of the 512 rows of one device at most 8 name the same owner, and in some blocks one owner is named by exactly 8 rows. `cell_element`: the element of a node held by the device with grp index g lies in g * 128 * 32 to (g + 1) * 128 * 32 - 1; element e is owned by the device at flattened index e // 128.
All inputs are finite; a program needn't handle non-finite values.
Results may differ from a plain program's by a relative error of at most 0.00002.
Values sent between devices are 32-bit elements; how exact they have to be, the bound alone decides.
A program may use at most 128 MiB of HBM per device.

v0:
```python
import math

import jax
import jax.numpy as jnp
from jax import lax
from jax.sharding import PartitionSpec as P

SWEEPS = 8
PICARD = 2


def padded_2(block, sides, width):
    for axis, dim in sides:
        count = lax.axis_size(axis)
        forward = [(i, i + 1) for i in range(count - 1)]
        backward = [(target, source) for source, target in forward]
        low = lax.ppermute(
            lax.slice_in_dim(block, block.shape[dim] - width, None, axis=dim), axis, forward
        )
        high = lax.ppermute(lax.slice_in_dim(block, 0, width, axis=dim), axis, backward)
        block = jnp.concatenate([low, block, high], axis=dim)
    return block


def grad_x(p):
    return 0.5 * (p[1:, 1:] + p[1:, :-1] - p[:-1, 1:] - p[:-1, :-1])


def grad_y(p):
    return 0.5 * (p[1:, 1:] + p[:-1, 1:] - p[1:, :-1] - p[:-1, :-1])


def spread_x(t):
    return 0.5 * (t[:-1, :-1] + t[:-1, 1:] - t[1:, :-1] - t[1:, 1:])


def spread_y(t):
    return 0.5 * (t[:-1, :-1] + t[1:, :-1] - t[:-1, 1:] - t[1:, 1:])


def corner_mean(e):
    return 0.25 * (e[1:, 1:] + e[1:, :-1] + e[:-1, 1:] + e[:-1, :-1])


def local_operate(padded, quad_visc, friction):
    values = padded[:, 1:-1, 1:-1]
    u_dx = grad_x(padded[0])
    u_dy = grad_y(padded[0])
    v_dx = grad_x(padded[1])
    v_dy = grad_y(padded[1])
    stress_xx = quad_visc * (4.0 * u_dx + 2.0 * v_dy)
    stress_yy = quad_visc * (4.0 * v_dy + 2.0 * u_dx)
    stress_xy = quad_visc * (u_dy + v_dx)
    first = spread_x(stress_xx) + spread_y(stress_xy) + friction * values[0]
    second = spread_y(stress_yy) + spread_x(stress_xy) + friction * values[1]
    return jnp.stack([first, second])


def operate(values, quad_visc, friction):
    padded = padded_2(values, (("grp", 1), ("tile", 2)), 1)
    return local_operate(padded, quad_visc, friction)


def row_gradient(look_x, look_y, observed, speed_x, speed_y, epochs):
    misfit_rows = look_x * speed_x[:, None] + look_y * speed_y[:, None] - observed
    first = jnp.sum(misfit_rows * look_x, axis=1)
    second = jnp.sum(misfit_rows * look_y, axis=1)
    return jnp.stack([first, second]) / math.sqrt(epochs)


def shards(
    start_velocity,
    driving_stress,
    viscosity,
    friction,
    cell_element,
    observed,
    look,
    row_owner,
    row_cell,
):
    rows_x, rows_y = friction.shape
    row_dev, epochs = observed.shape
    devices = lax.axis_size("grp") * lax.axis_size("tile")
    capacity = max(2, 2 * row_dev // devices)
    owner_dev = row_owner[:, 0]
    owner_marks = (owner_dev[:, None] == jnp.arange(devices, dtype=jnp.int32)[None, :]).astype(
        jnp.int32
    )
    slot_rank = jnp.sum((jnp.cumsum(owner_marks, axis=0) - owner_marks) * owner_marks, axis=1)
    row_slot = owner_dev * capacity + slot_rank
    slot_cells = (
        jnp.zeros((devices * capacity,), jnp.int32)
        .at[row_slot]
        .set(row_cell)
        .reshape(devices, capacity)
    )
    packed = jnp.concatenate([look, observed[None]], axis=0)
    outgoing = jnp.zeros((3, devices * capacity, epochs), jnp.float32).at[:, row_slot].set(packed)
    arrived = lax.all_to_all(
        outgoing.reshape(3, devices, capacity, epochs),
        ("grp", "tile"),
        split_axis=1,
        concat_axis=1,
        tiled=True,
    )
    arrived = arrived.reshape(3, devices * capacity, epochs)
    arrived_cells = lax.all_to_all(
        slot_cells, ("grp", "tile"), split_axis=0, concat_axis=0, tiled=True
    ).reshape(-1)
    saved = []
    prec_list = []
    diag_list = []
    visc_rim = padded_2(viscosity, (("grp", 1), ("tile", 2)), 1)
    quad_list = []
    for picard in range(PICARD):
        quad_visc = corner_mean(visc_rim[picard])
        diagonal = (
            1.25
            * (quad_visc[:-1, :-1] + quad_visc[:-1, 1:] + quad_visc[1:, :-1] + quad_visc[1:, 1:])
            + friction
        )
        quad_list.append(quad_visc)
        diag_list.append(diagonal)
        prec_list.append(0.45 / diagonal)
    velocity = start_velocity
    for picard in range(PICARD):
        for _ in range(SWEEPS):
            residual = driving_stress - operate(velocity, quad_list[picard], friction)
            saved.append((velocity, residual))
            velocity = velocity + prec_list[picard] * residual
    flat_velocity = velocity.reshape(2, rows_x * rows_y)
    speeds = flat_velocity[:, arrived_cells]
    row_grads = row_gradient(arrived[0], arrived[1], arrived[2], speeds[0], speeds[1], epochs)
    adjoint = jnp.zeros((2, rows_x * rows_y), jnp.float32).at[:, arrived_cells].add(row_grads)
    adjoint = adjoint.reshape(2, rows_x, rows_y)
    stress_adjoint = jnp.zeros_like(driving_stress)
    friction_grad = jnp.zeros_like(friction)
    for position in range(len(saved) - 1, -1, -1):
        velocity_in, residual = saved[position]
        picard = position // SWEEPS
        precond = prec_list[picard]
        scaled = precond * adjoint
        stress_adjoint = stress_adjoint + scaled
        friction_grad = friction_grad - (scaled[0] * velocity_in[0] + scaled[1] * velocity_in[1])
        friction_grad = friction_grad - precond / diag_list[picard] * (
            adjoint[0] * residual[0] + adjoint[1] * residual[1]
        )
        if position > 0:
            adjoint = adjoint - operate(scaled, quad_list[picard], friction)
    node_terms = (friction * friction_grad).reshape(-1)
    elem_dev = rows_x * rows_y // 128
    group_width = elem_dev * lax.axis_size("tile")
    first_element = lax.axis_index("grp") * group_width
    local_ids = cell_element.reshape(-1) - first_element
    element_terms = jnp.zeros((group_width,), jnp.float32).at[local_ids].add(node_terms)
    friction_adjoint = lax.psum_scatter(element_terms, "tile", scatter_dimension=0, tiled=True)
    return (stress_adjoint, friction_adjoint)


def solution(mesh):
    return jax.shard_map(
        shards,
        mesh=mesh,
        in_specs=(
            P(None, "grp", "tile"),
            P(None, "grp", "tile"),
            P(None, "grp", "tile"),
            P("grp", "tile"),
            P("grp", "tile"),
            P(("grp", "tile"), None),
            P(None, ("grp", "tile"), None),
            P(("grp", "tile"), None),
            P(("grp", "tile")),
        ),
        out_specs=(P(None, "grp", "tile"), P(("grp", "tile"))),
        check_vma=False,
    )
```

profile of v0, /device:TPU:32, one launch (start us, length us, event | category | flops | bytes accessed | tf_op | source)
XLA Modules:
  0.0 1063.4 jit_solution(7330825783483209055)
XLA Ops:
  21.4 6.1 collective-permute-start.2
  134.0 5.7 collective-permute-done.27
  148.0 6.3 collective-permute-start.30
  156.0 5.7 collective-permute-done.31
  170.0 6.3 collective-permute-start.34
  305.5 14.1 %all-to-all-start = ((s32[128,1,8]{2,1,0:T(1,128)}), s32[128,1,8]{2,1,0:T(1,128)}, u32[]{:S(2)}, u32[]{:S(2)}) async-start(s32[128,1,8]{2,1,0:T(1,128)} %bitcast.8), calls=%async_computation | async-start | bytes 131072 | tf_op jit(solution)/shard_map/all_to_all | solution.py:108
  332.0 47.5 %scatter_fusion = f32[3,1024,256]{2,0,1:T(4,128)} fusion(f32[3,1024,256]{2,0,1:T(4,128)} %broadcast_in_dim.11, s32[512]{0:T(512)} %bitcast.862, f32[512,3,256]{2,1,0:T(4,128)S(1)} %copy.26), kind=kCustom, calls=%fused_computation.2 | custom fusion | bytes 4720640 | tf_op jit(solution)/shard_map/scatter | solution.py:99
  390.1 11.6 %all-to-all-start.1 = ((f32[3,128,8,256]{3,2,0,1:T(8,128)}), f32[3,128,8,256]{3,2,0,1:T(8,128)}, u32[]{:S(2)}, u32[]{:S(2)}) async-start(f32[3,128,8,256]{3,2,0,1:T(8,128)} %copy.27), calls=%async_computation.1 | async-start | bytes 6291456 | tf_op jit(solution)/shard_map/all_to_all | solution.py:100
  418.2 20.4 %collective-permute-done.66 = f32[2,34,1]{2,1,0:T(8,128)S(1)} collective-permute-done((f32[2,34,1]{2,1,0:T(8,128)S(1)}, f32[2,34,1]{2,1,0:T(8,128)S(1)}, u32[]{:S(2)}, u32[]{:S(2)}) %collective-permute-start.66) | collective-permute-done | bytes 304 | tf_op jit(solution)/shard_map/ppermute | solution.py:17
  444.6 6.2 gather_fusion
  454.5 9.8 scatter_custom_fusion.2
  476.6 6.1 collective-permute-start.70
  523.9 5.7 collective-permute-done.79
  537.3 6.3 collective-permute-start.82
  545.3 5.7 collective-permute-done.83
  558.6 6.3 collective-permute-start.86
  585.8 5.7 collective-permute-done.91
  599.2 6.3 collective-permute-start.94
  607.2 5.7 collective-permute-done.95
  620.6 6.3 collective-permute-start.98
  683.0 6.3 collective-permute-start.110
  763.6 13.0 %slice_reduce_fusion.1 = (f32[16384]{0:T(1024)}, f32[16384]{0:T(1024)S(1)}) fusion(f32[2,16384]{0,1:T(8,128)} %scatter_custom_fusion.2), kind=kLoop, calls=%fused_computation.6 | loop fusion | bytes 262144 | tf_op jit(solution)/shard_map/slice | solution.py:147
  797.9 86.0 %scatter_custom_fusion.3 = f32[4096]{0:T(1024)S(1)} fusion(s32[16384]{0:T(1024)} %bitcast.854, f32[16384]{0:T(1024)S(1)} %bitcast.855, f32[]{:T(128)} %constant.158.clone.1), kind=kCustom, calls=%fused_computation.1076 | custom fusion | flops 16384 | bytes 16896 | tf_op jit(solution)/shard_map/scatter-add | solution.py:156
  883.9 178.5 %all-reduce = f32[4096]{0:T(1024)S(1)} all-reduce(f32[4096]{0:T(1024)S(1)} %scatter_custom_fusion.3), channel_id=2, replica_groups=mesh['grp'=4,'tile'=32] {'tile'}, use_global_device_ids=true, to_apply=%region_9.10.clone | all-reduce | flops 4096 | bytes 32768
  (689 shorter events, 579.8 us)
Async XLA Ops:
  1.5 11.9 %collective-permute-start.4 = (f32[2,1,512]{2,1,0:T(1,128)S(1)}, f32[2,1,512]{2,1,0:T(1,128)S(1)}, u32[]{:S(2)}, u32[]{:S(2)}) collective-permute-start(f32[2,1,512]{2,1,0:T(1,128)S(1)} %get-tuple-element.451), channel_id=1, source_target_pairs={{0,32},{32,64},{64,96},{1,33},{33,65},{65,97},{2,34},{34,66},{66,9... | collective-permute-start | bytes 12296 | tf_op jit(solution)/shard_map/ppermute | solution.py:17
  3.4 10.0 collective-permute-start.5
  7.8 12.7 %collective-permute-start = (f32[2,1,512]{2,1,0:T(1,128)S(1)}, f32[2,1,512]{2,1,0:T(1,128)S(1)}, u32[]{:S(2)}, u32[]{:S(2)}) collective-permute-start(f32[2,1,512]{2,1,0:T(1,128)S(1)} %get-tuple-element.449), channel_id=1, source_target_pairs={{0,32},{32,64},{64,96},{1,33},{33,65},{65,97},{2,34},{34,66},{66,9... | collective-permute-start | bytes 12296 | tf_op jit(solution)/shard_map/ppermute | solution.py:17
  9.8 10.7 %collective-permute-start.1 = (f32[2,1,512]{2,1,0:T(1,128)S(1)}, f32[2,1,512]{2,1,0:T(1,128)S(1)}, u32[]{:S(2)}, u32[]{:S(2)}) collective-permute-start(f32[2,1,512]{2,1,0:T(1,128)S(1)} %get-tuple-element.450), channel_id=1, source_target_pairs={{32,0},{64,32},{96,64},{33,1},{65,33},{97,65},{34,2},{66,34},{98,6... | collective-permute-start | bytes 12296 | tf_op jit(solution)/shard_map/ppermute | solution.py:20
  14.3 14.4 %collective-permute-start.6 = (f32[2,34,1]{2,1,0:T(8,128)S(1)}, f32[2,34,1]{2,1,0:T(8,128)S(1)}, u32[]{:S(2)}, u32[]{:S(2)}) collective-permute-start(f32[2,34,1]{2,1,0:T(8,128)S(1)} %get-tuple-element.387), channel_id=1, source_target_pairs={{0,1},{1,2},{2,3},{3,4},{4,5},{5,6},{6,7},{7,8},{8,9},{9,10},{10,1... | collective-permute-start | bytes 824 | tf_op jit(solution)/shard_map/ppermute | solution.py:17
  19.2 9.6 collective-permute-start.7
  21.4 8.5 collective-permute-start.2
  148.0 8.0 collective-permute-start.30
  170.0 8.0 collective-permute-start.34
  296.0 23.6 %collective-permute-start.58 = (f32[2,34,1]{2,1,0:T(8,128)S(1)}, f32[2,34,1]{2,1,0:T(8,128)S(1)}, u32[]{:S(2)}, u32[]{:S(2)}) collective-permute-start(f32[2,34,1]{2,1,0:T(8,128)S(1)} %get-tuple-element.359), channel_id=1, source_target_pairs={{0,1},{1,2},{2,3},{3,4},{4,5},{5,6},{6,7},{7,8},{8,9},{9,10},{10,1... | collective-permute-start | bytes 824 | tf_op jit(solution)/shard_map/ppermute | solution.py:17
  300.9 18.7 %collective-permute-start.59 = (f32[2,34,1]{2,1,0:T(8,128)S(1)}, f32[2,34,1]{2,1,0:T(8,128)S(1)}, u32[]{:S(2)}, u32[]{:S(2)}) collective-permute-start(f32[2,34,1]{2,1,0:T(8,128)S(1)} %get-tuple-element.360), channel_id=1, source_target_pairs={{1,0},{2,1},{3,2},{4,3},{5,4},{6,5},{7,6},{8,7},{9,8},{10,9},{11,1... | collective-permute-start | bytes 824 | tf_op jit(solution)/shard_map/ppermute | solution.py:20
  305.5 84.6 %all-to-all-start = ((s32[128,1,8]{2,1,0:T(1,128)}), s32[128,1,8]{2,1,0:T(1,128)}, u32[]{:S(2)}, u32[]{:S(2)}) async-start(s32[128,1,8]{2,1,0:T(1,128)} %bitcast.8), calls=%async_computation | async-start | bytes 131072 | tf_op jit(solution)/shard_map/all_to_all | solution.py:108
  321.6 62.5 %collective-permute-start.60 = (f32[2,1,512]{2,1,0:T(1,128)}, f32[2,1,512]{2,1,0:T(1,128)S(1)}, u32[]{:S(2)}, u32[]{:S(2)}) collective-permute-start(f32[2,1,512]{2,1,0:T(1,128)} %get-tuple-element.421), channel_id=1, source_target_pairs={{0,32},{32,64},{64,96},{1,33},{33,65},{65,97},{2,34},{34,66},{66,9... | collective-permute-start | bytes 12296 | tf_op jit(solution)/shard_map/ppermute | solution.py:17
  323.6 60.5 %collective-permute-start.61 = (f32[2,1,512]{2,1,0:T(1,128)}, f32[2,1,512]{2,1,0:T(1,128)S(1)}, u32[]{:S(2)}, u32[]{:S(2)}) collective-permute-start(f32[2,1,512]{2,1,0:T(1,128)} %get-tuple-element.422), channel_id=1, source_target_pairs={{32,0},{64,32},{96,64},{33,1},{65,33},{97,65},{34,2},{66,34},{98,6... | collective-permute-start | bytes 12296 | tf_op jit(solution)/shard_map/ppermute | solution.py:20
  384.2 19.8 %collective-permute-start.62 = (f32[2,34,1]{2,1,0:T(8,128)S(1)}, f32[2,34,1]{2,1,0:T(8,128)S(1)}, u32[]{:S(2)}, u32[]{:S(2)}) collective-permute-start(f32[2,34,1]{2,1,0:T(8,128)S(1)} %get-tuple-element.357), channel_id=1, source_target_pairs={{0,1},{1,2},{2,3},{3,4},{4,5},{5,6},{6,7},{7,8},{8,9},{9,10},{10,1... | collective-permute-start | bytes 824 | tf_op jit(solution)/shard_map/ppermute | solution.py:17
  388.8 15.1 %collective-permute-start.63 = (f32[2,34,1]{2,1,0:T(8,128)S(1)}, f32[2,34,1]{2,1,0:T(8,128)S(1)}, u32[]{:S(2)}, u32[]{:S(2)}) collective-permute-start(f32[2,34,1]{2,1,0:T(8,128)S(1)} %get-tuple-element.358), channel_id=1, source_target_pairs={{1,0},{2,1},{3,2},{4,3},{5,4},{6,5},{7,6},{8,7},{9,8},{10,9},{11,1... | collective-permute-start | bytes 824 | tf_op jit(solution)/shard_map/ppermute | solution.py:20
  390.1 61.3 %all-to-all-start.1 = ((f32[3,128,8,256]{3,2,0,1:T(8,128)}), f32[3,128,8,256]{3,2,0,1:T(8,128)}, u32[]{:S(2)}, u32[]{:S(2)}) async-start(f32[3,128,8,256]{3,2,0,1:T(8,128)} %copy.27), calls=%async_computation.1 | async-start | bytes 6291456 | tf_op jit(solution)/shard_map/all_to_all | solution.py:100
  412.2 26.4 %collective-permute-start.66 = (f32[2,34,1]{2,1,0:T(8,128)S(1)}, f32[2,34,1]{2,1,0:T(8,128)S(1)}, u32[]{:S(2)}, u32[]{:S(2)}) collective-permute-start(f32[2,34,1]{2,1,0:T(8,128)S(1)} %get-tuple-element.355), channel_id=1, source_target_pairs={{0,1},{1,2},{2,3},{3,4},{4,5},{5,6},{6,7},{7,8},{8,9},{9,10},{10,1... | collective-permute-start | bytes 824 | tf_op jit(solution)/shard_map/ppermute | solution.py:17
  416.8 21.9 %collective-permute-start.67 = (f32[2,34,1]{2,1,0:T(8,128)S(1)}, f32[2,34,1]{2,1,0:T(8,128)S(1)}, u32[]{:S(2)}, u32[]{:S(2)}) collective-permute-start(f32[2,34,1]{2,1,0:T(8,128)S(1)} %get-tuple-element.356), channel_id=1, source_target_pairs={{1,0},{2,1},{3,2},{4,3},{5,4},{6,5},{7,6},{8,7},{9,8},{10,9},{11,1... | collective-permute-start | bytes 824 | tf_op jit(solution)/shard_map/ppermute | solution.py:20
  537.3 8.0 collective-permute-start.82
  599.2 8.0 collective-permute-start.94
  758.0 18.6 %collective-permute-start.124 = (f32[2,1,512]{2,1,0:T(1,128)S(1)}, f32[2,1,512]{2,1,0:T(1,128)S(1)}, u32[]{:S(2)}, u32[]{:S(2)}) collective-permute-start(f32[2,1,512]{2,1,0:T(1,128)S(1)} %get-tuple-element.389), channel_id=1, source_target_pairs={{0,32},{32,64},{64,96},{1,33},{33,65},{65,97},{2,34},{34,66},{66,9... | collective-permute-start | bytes 12296 | tf_op jit(solution)/shard_map/ppermute | solution.py:17
  759.9 16.7 %collective-permute-start.125 = (f32[2,1,512]{2,1,0:T(1,128)S(1)}, f32[2,1,512]{2,1,0:T(1,128)S(1)}, u32[]{:S(2)}, u32[]{:S(2)}) collective-permute-start(f32[2,1,512]{2,1,0:T(1,128)S(1)} %get-tuple-element.390), channel_id=1, source_target_pairs={{32,0},{64,32},{96,64},{33,1},{65,33},{97,65},{34,2},{66,34},{98,6... | collective-permute-start | bytes 12296 | tf_op jit(solution)/shard_map/ppermute | solution.py:20
  777.4 9.5 collective-permute-start.126
  (182 other events, 2328.5 us)
where the time goes:
time: 1080 us; the launch traced here: 1060 us
  starting transfers between devices  415 us (38%)
  waiting for transfers between devices  221 us (20%)
  blocking collectives  179 us (17%)
  other arithmetic  147 us (14%)
  local copies, waits for them, and re-layouts  96.7 us (9%)
    ppermute x64, starting transfers between devices, padded_2(): lax.ppermute(lax.slice_in_dim(block, block.shape[dim] - width, None, axis...  230 us
    ppermute x64, waiting for transfers between devices, padded_2(): lax.ppermute(lax.slice_in_dim(block, 0, width, axis=dim), axis, backward)  192 us
    unnamed x1, blocking collectives  179 us
    ppermute x64, starting transfers between devices, padded_2(): lax.ppermute(lax.slice_in_dim(block, 0, width, axis=dim), axis, backward)  159 us
    scatter-add x1, other arithmetic, shards(): jnp.zeros((group_width,), jnp.float32).at[local_ids].add(node_terms)  86 us
    scatter x1, local copies, waits for them, and re-layouts, shards(): jnp.zeros((3, devices * capacity, epochs), jnp.float32).at[:, row_slot]  47.5 us
    ppermute x64, waiting for transfers between devices, padded_2(): lax.ppermute(lax.slice_in_dim(block, block.shape[dim] - width, None, axis...  28.5 us
  transfers between devices with their start and end apart: 130, of which 81 were waited for; matrix products, arithmetic and copies ran while one was open for 9% of the time, Pallas kernels for 0%

commit v1 on v0

v1 whole, which is shorter than its diff:
```python
import functools

import jax
import jax.numpy as jnp
from jax import lax
from jax.experimental import pallas as pl
from jax.experimental.pallas import tpu as pltpu
from jax.sharding import PartitionSpec as P

MESH = pl.DeviceIdType.MESH
CX, CY = 32, 512
SWEEPS, PICARD = 8, 2
STEPS = SWEEPS * PICARD
W = 16
EX = CX + 2 * W
SEG = 8
LANES = 128
NF = 7
SLOTS = 8
F32, BF16, I32 = jnp.float32, jnp.bfloat16, jnp.int32
FORWARD = ((0, 4), (4, 4), (8, 4), (12, 4))
BACKWARD = ((0, 4), (4, 4), (8, 4), (12, 3))


def roll(x, amount):
    return pltpu.roll(x, amount % LANES, 1)


def right(x):
    return roll(x, -1)


def left(x):
    return roll(x, 1)


def pieces(x):
    high = x.astype(BF16)
    rest = x - high.astype(F32)
    middle = rest.astype(BF16)
    return high, middle, (rest - middle.astype(F32)).astype(BF16)


def iota(shape, dim):
    return lax.broadcasted_iota(I32, shape, dim)


def rows_kernel(n_grp, n_tile, look, observed, owner, cell, out):
    rows, epochs = observed.shape
    devices = n_grp * n_tile
    owner_row = owner[...]
    lane = iota((rows, LANES), 1)
    owner_col = jnp.transpose(jnp.broadcast_to(owner_row.astype(F32), (LANES, rows)))
    cell_col = jnp.transpose(jnp.broadcast_to(cell[...].astype(F32), (LANES, rows)))
    mark = owner_col == lane.astype(F32)
    marks = jnp.where(mark, 1.0, 0.0)
    below = jnp.where(iota((rows, rows), 0) > iota((rows, rows), 1), 1.0, 0.0).astype(BF16)
    before = jnp.dot(below, marks.astype(BF16), preferred_element_type=F32)
    rank = jnp.sum(before * marks, axis=1, keepdims=True)
    x, y, o = look[0], look[1], observed[...]
    sums = [jnp.sum(a * b, axis=1, keepdims=True) for a, b in ((x, x), (x, y), (y, y), (x, o), (y, o))]
    value = cell_col
    for j, part in enumerate(sums):
        value = jnp.where(lane >= SLOTS * (j + 1), part, value)
    keep = (rank == (lane % SLOTS).astype(F32)) & (lane < SLOTS * 6)
    value = jnp.where(keep, value, 0.0)
    place = owner_row % n_tile * 8 + owner_row // n_tile
    chosen = jnp.where(iota((n_tile * 8, rows), 0) == place, 1.0, 0.0).astype(BF16)
    total = sum(jnp.dot(chosen, piece, preferred_element_type=F32) for piece in pieces(value))
    out[...] = total.reshape(n_tile, 8, LANES)


def main_kernel(
    n_grp, n_tile,
    vel, stress, visc, fric, elem, outgoing,
    stress_out, elem_out,
    edge_l, edge_r, halo_t, halo_b, halo_l, halo_r,
    adj_n, adj_t, adj_b, aedge_l, aedge_r, ahalo_l, ahalo_r,
    first_r, second_s, second_r, gram_a, gram_b, gram,
    fields, half_q, quart_q, prec, keep_c, drive_u, drive_v,
    moments, adj, grads, grad_n, one_lo, elem_s, elem_r,
    send_sem, recv_sem, asend_sem, arecv_sem, row_send, row_recv, grp_send, grp_recv, el_send, el_recv,
):
    g, t = lax.axis_index("grp"), lax.axis_index("tile")
    fields2 = fields.reshape(NF * EX * SEG, LANES)
    lane8 = iota((8, LANES), 1)

    barrier = pltpu.get_barrier_semaphore()
    for ref in (halo_t, halo_b, halo_l, halo_r, adj_t, adj_b, ahalo_l, ahalo_r):
        ref[...] = jnp.zeros_like(ref)

    def greet(device):
        pl.semaphore_signal(barrier, inc=1, device_id=device, device_id_type=MESH)

    up, down, west, east = g > 0, g < n_grp - 1, t > 0, t < n_tile - 1
    for step in range(1, n_grp):
        greet((lax.rem(g + step, n_grp), t))

    def greet_tile(step, carry):
        greet((g, lax.rem(t + step, n_tile)))
        return carry

    lax.fori_loop(1, n_tile, greet_tile, 0)
    diagonals = ((up & west, -1, -1), (up & east, -1, 1), (down & west, 1, -1), (down & east, 1, 1))
    total = n_grp - 1 + n_tile - 1
    for there, dg, dt in diagonals:
        pl.when(there)(functools.partial(greet, (g + dg, t + dt)))
        total = total + there.astype(I32)

    natural = [(vel, 0), (vel, 1), (stress, 0), (stress, 1), (visc, 0), (visc, 1), (fric, None)]

    def tile_of(f, r, m):
        ref, index = natural[f]
        where = (pl.ds(8 * r, 8), pl.ds(LANES * m, LANES))
        return ref[where] if index is None else ref[(index,) + where]

    for r in range(CX // 8):
        low, high = None, None
        for f in range(NF):
            a = roll(tile_of(f, r, 0), 16 * f)
            b = roll(tile_of(f, r, CY // LANES - 1), 16 * f + 16)
            low = a if low is None else jnp.where(lane8 >= 16 * f, a, low)
            high = b if high is None else jnp.where(lane8 >= 16 * f, b, high)
        edge_l[pl.ds(8 * r, 8), :] = low
        edge_r[pl.ds(8 * r, 8), :] = high

    pl.semaphore_wait(barrier, total)

    def neighbours(blocks, e_l, e_r, h_l, h_r, send, recv):
        moves = []
        for ref, h_t, h_b in blocks:
            moves.append((down, up, ref(W), h_t, (g + 1, t)))
            moves.append((up, down, ref(0), h_b, (g - 1, t)))
        moves.append((east, west, e_r, h_l.at[pl.ds(W, CX)], (g, t + 1)))
        moves.append((west, east, e_l, h_r.at[pl.ds(W, CX)], (g, t - 1)))
        last, head, foot = pl.ds(W, W), pl.ds(0, W), pl.ds(W + CX, W)
        moves.append((down & east, up & west, e_r.at[last], h_l.at[head], (g + 1, t + 1)))
        moves.append((up & east, down & west, e_r.at[head], h_l.at[foot], (g - 1, t + 1)))
        moves.append((down & west, up & east, e_l.at[last], h_r.at[head], (g + 1, t - 1)))
        moves.append((up & west, down & east, e_l.at[head], h_r.at[foot], (g - 1, t - 1)))
        out = []
        for i, (sends, gets, source, target, device) in enumerate(moves):
            copy = pltpu.make_async_remote_copy(
                src_ref=source, dst_ref=target, send_sem=send.at[i], recv_sem=recv.at[i],
                device_id=device, device_id_type=MESH,
            )
            out.append((sends, gets, copy))
        return out

    def begin(moves):
        for sends, _, copy in moves:
            pl.when(sends)(copy.start)

    def arrive(moves):
        for _, gets, copy in moves:
            pl.when(gets)(copy.wait_recv)

    def leave(moves):
        for sends, _, copy in moves:
            pl.when(sends)(copy.wait_send)

    def rows_of(ref):
        if len(ref.shape) == 2:
            return lambda start: ref.at[pl.ds(start, W), :]
        return lambda start: ref.at[:, pl.ds(start, W), :]

    moves = neighbours(
        [
            (rows_of(vel), halo_t.at[pl.ds(0, 2)], halo_b.at[pl.ds(0, 2)]),
            (rows_of(stress), halo_t.at[pl.ds(2, 2)], halo_b.at[pl.ds(2, 2)]),
            (rows_of(visc), halo_t.at[pl.ds(4, 2)], halo_b.at[pl.ds(4, 2)]),
            (rows_of(fric), halo_t.at[6], halo_b.at[6]),
        ],
        edge_l, edge_r, halo_l, halo_r, send_sem, recv_sem,
    )
    begin(moves)

    def send_rows(step, carry):
        to = lax.rem(t + step, n_tile)
        pltpu.make_async_remote_copy(
            src_ref=outgoing.at[to], dst_ref=first_r.at[t], send_sem=row_send, recv_sem=row_recv,
            device_id=(g, to), device_id_type=MESH,
        ).start()
        return carry

    lax.fori_loop(1, n_tile, send_rows, 0)

    first_element = g * (n_tile * LANES)
    for r in range(CX):
        low = (elem[pl.ds(r, 1), :] - first_element) % LANES
        one_lo[r] = jnp.where(iota((LANES, CY), 0) == low, 1.0, 0.0).astype(BF16)

    def spread(target, base, row, tiles, before, after):
        wide = [roll(x, 32) for x in tiles]
        back = [roll(x, -32) for x in tiles]
        for m in range(CY // LANES):
            even = jnp.where(lane8 < 32, before if m == 0 else wide[m - 1], wide[m])
            odd = jnp.where(lane8 < 96, back[m], after if m == CY // LANES - 1 else back[m + 1])
            target[pl.ds((base + row) * SEG + 2 * m, 8, stride=SEG), :] = even
            target[pl.ds((base + row) * SEG + 2 * m + 1, 8, stride=SEG), :] = odd

    def spread_block(f, r, tiles):
        at = pl.ds(8 * r, 8)
        spread(
            fields2, f * EX, 8 * r, tiles,
            roll(halo_l[at, :], 16 - 16 * f), roll(halo_r[at, :], 96 - 16 * f),
        )

    arrive(moves)
    for f in range(NF):
        for r in range(EX // 8):
            if r < W // 8:
                tiles = [halo_t[f, pl.ds(8 * r, 8), pl.ds(LANES * m, LANES)] for m in range(4)]
            elif r >= (W + CX) // 8:
                k = r - (W + CX) // 8
                tiles = [halo_b[f, pl.ds(8 * k, 8), pl.ds(LANES * m, LANES)] for m in range(4)]
            else:
                tiles = [tile_of(f, r - W // 8, m) for m in range(4)]
            spread_block(f, r, tiles)

    seg8 = iota((SEG, LANES), 0)
    inside = ((t > 0) | (seg8 > 0) | (lane8 >= 32)) & ((t < n_tile - 1) | (seg8 < SEG - 1) | (lane8 < 96))
    inside_top = inside & up
    inside_bottom = inside & down
    for p in range(PICARD):
        pair = fields[4 + p, 0]
        pair = pair + right(pair)
        q_old = None
        for k in range(EX - 1):
            other = fields[4 + p, k + 1]
            other = other + right(other)
            q = 0.25 * (pair + other)
            pair = other
            half_q[p, k] = 0.5 * q
            quart_q[p, k] = 0.25 * q
            if q_old is not None:
                both = q_old + q
                b = fields[6, k]
                diagonal = 1.25 * (both + left(both)) + b
                mask = inside_top if k < W else inside_bottom if k >= W + CX else inside
                c = jnp.where(mask, 0.45 / diagonal, 0.0)
                prec[p, k] = c
                keep_c[p, k] = jnp.where(mask, 1.0 - c * b, 0.0)
                drive_u[p, k] = c * fields[2, k]
                drive_v[p, k] = c * fields[3, k]
            q_old = q

    def stencil(load, p, lo, hi, use):
        prev, stress_prev = None, None
        for k in range(lo - 1, hi + 2):
            a, b = load(k)
            la, lb = right(a), right(b)
            xa, yb = a + la, lb - b
            ya, xb = la - a, b + lb
            plus, minus = ya + xb, ya - xb
            now = None
            if prev is not None:
                xm = xa - prev[0]
                ym = yb + prev[1]
                sh = plus + prev[2]
                both = xm + ym
                h = half_q[p, k - 1]
                now = (h * (both + xm), h * (both + ym), quart_q[p, k - 1] * sh)
                if stress_prev is not None:
                    dxx = stress_prev[0] - now[0]
                    myy = stress_prev[1] + now[1]
                    mxy = stress_prev[2] + now[2]
                    dxy = stress_prev[2] - now[2]
                    use(k - 1, (dxx - mxy) + left(dxx + mxy), (dxy - myy) + left(dxy + myy), prev[3], prev[4])
            prev, stress_prev = (xa, yb, minus, a, b), now

    inv = 1.0 / 0.45

    def forward(start, count):
        p = start // SWEEPS
        lo, hi = start + 1, EX - 2 - start

        def sweep(s, carry):
            def use(k, first, second, u, v):
                c, d = prec[p, k], keep_c[p, k]
                new_u = (d * u + drive_u[p, k]) - c * first
                new_v = (d * v + drive_v[p, k]) - c * second
                fields[0, k] = new_u
                fields[1, k] = new_v
                if W <= k < W + CX:
                    moments[s, 0, k - W] = inv * new_u + (1.0 - inv) * u
                    moments[s, 1, k - W] = inv * new_v + (1.0 - inv) * v

            stencil(lambda k: (fields[0, k], fields[1, k]), p, lo, hi, use)
            return carry

        lax.fori_loop(start, start + count, sweep, 0)

    for start, count in FORWARD[:2]:
        forward(start, count)

    everyone = pl.ds(0, n_tile - 1)
    pltpu.make_async_remote_copy(
        src_ref=outgoing.at[everyone], dst_ref=first_r.at[everyone], send_sem=row_send, recv_sem=row_recv,
        device_id=(g, t), device_id_type=MESH,
    ).wait()
    own = outgoing[t]
    first_r[t] = own
    flat_r = first_r.reshape(n_tile * 8, LANES)
    for k in range(n_grp):
        second_s[k] = flat_r[pl.ds(k, n_tile, stride=8), :]
    second_r[g] = second_s[g]

    def group_copy(step):
        to = lax.rem(g + step, n_grp)
        return pltpu.make_async_remote_copy(
            src_ref=second_s.at[to], dst_ref=second_r.at[g], send_sem=grp_send.at[step - 1],
            recv_sem=grp_recv.at[step - 1], device_id=(to, t), device_id_type=MESH,
        )

    for step in range(1, n_grp):
        group_copy(step).start()

    forward(*FORWARD[2])

    for step in range(1, n_grp):
        group_copy(step).wait()
    sources = n_grp * n_tile
    arrived = jnp.transpose(second_r[...].reshape(sources, LANES))
    for s in range(SLOTS):
        cell = arrived[s : s + 1, :].astype(I32)
        at = pl.ds(s * sources, sources)
        gram_b[:, at] = jnp.where(iota((CY, sources), 0) == cell % CY, 1.0, 0.0).astype(BF16)
        chosen = iota((CX, sources), 0) == cell // CY
        for j in range(5):
            row = SLOTS * (j + 1) + s
            value = jnp.where(chosen, arrived[row : row + 1, :], 0.0)
            for q, piece in enumerate(pieces(value)):
                gram_a[pl.ds((q * 5 + j) * CX, CX), at] = piece
    product = lax.dot_general(
        gram_a[...], gram_b[...], (((1,), (1,)), ((), ())), preferred_element_type=F32
    )
    part = 5 * CX
    gram[...] = product[:part] + product[part : 2 * part] + product[2 * part :]

    forward(*FORWARD[3])

    def collect(source, base, r, m):
        a = source[pl.ds(base * SEG + 8 * SEG * r + 2 * m, 8, stride=SEG), :]
        b = source[pl.ds(base * SEG + 8 * SEG * r + 2 * m + 1, 8, stride=SEG), :]
        return jnp.where(lane8 < 64, roll(a, -32), roll(b, 32))

    scale = 1.0 / 16.0
    for r in range(CX // 8):
        for m in range(CY // LANES):
            u = collect(fields2, W, r, m)
            v = collect(fields2, EX + W, r, m)
            at = pl.ds(LANES * m, LANES)
            sxx, sxy, syy, sxo, syo = [gram[pl.ds(j * CX + 8 * r, 8), at] for j in range(5)]
            adj_n[0, pl.ds(8 * r, 8), at] = scale * (sxx * u + sxy * v - sxo)
            adj_n[1, pl.ds(8 * r, 8), at] = scale * (sxy * u + syy * v - syo)
        rows = pl.ds(8 * r, 8)
        aedge_l[rows, :] = jnp.where(
            lane8 < 16, adj_n[0, rows, pl.ds(0, LANES)], roll(adj_n[1, rows, pl.ds(0, LANES)], 16)
        )
        end = pl.ds(CY - LANES, LANES)
        aedge_r[rows, :] = jnp.where(
            lane8 < 16, roll(adj_n[0, rows, end], 16), roll(adj_n[1, rows, end], 32)
        )
    amoves = neighbours(
        [(rows_of(adj_n), adj_t, adj_b)], aedge_l, aedge_r, ahalo_l, ahalo_r, asend_sem, arecv_sem
    )
    begin(amoves)
    grads[...] = jnp.zeros_like(grads)
    arrive(amoves)
    adj2 = adj.reshape(2 * EX * SEG, LANES)
    for f in range(2):
        for r in range(EX // 8):
            if r < W // 8:
                source, k = adj_t, r
            elif r >= (W + CX) // 8:
                source, k = adj_b, r - (W + CX) // 8
            else:
                source, k = adj_n, r - W // 8
            tiles = [source[f, pl.ds(8 * k, 8), pl.ds(LANES * m, LANES)] for m in range(4)]
            at = pl.ds(8 * r, 8)
            spread(
                adj2, f * EX, 8 * r, tiles,
                roll(ahalo_l[at, :], 16 - 16 * f), roll(ahalo_r[at, :], 96 - 16 * f),
            )

    def gather(position, k, a, b):
        i = k - W
        grads[0, i] = grads[0, i] + a
        grads[1, i] = grads[1, i] + b
        grads[2, i] = grads[2, i] - (a * moments[position, 0, i] + b * moments[position, 1, i])

    def backward(start, count):
        p = (STEPS - 1 - start) // SWEEPS
        lo, hi = start + 2, EX - 3 - start

        def sweep(s, carry):
            def load(k):
                c = prec[p, k]
                a, b = c * adj[0, k], c * adj[1, k]
                if W <= k < W + CX:
                    gather(STEPS - 1 - s, k, a, b)
                return a, b

            def use(k, first, second, a, b):
                d = keep_c[p, k]
                adj[0, k] = d * adj[0, k] - first
                adj[1, k] = d * adj[1, k] - second

            stencil(load, p, lo, hi, use)
            return carry

        lax.fori_loop(start, start + count, sweep, 0)

    for start, count in BACKWARD:
        backward(start, count)
    for k in range(W, W + CX):
        c = prec[0, k]
        gather(0, k, c * adj[0, k], c * adj[1, k])

    grads2 = grads.reshape(3 * CX * SEG, LANES)
    for r in range(CX // 8):
        for m in range(CY // LANES):
            rows, at = pl.ds(8 * r, 8), pl.ds(LANES * m, LANES)
            stress_out[0, rows, at] = collect(grads2, 0, r, m)
            stress_out[1, rows, at] = collect(grads2, CX, r, m)
            grad_n[rows, at] = fric[rows, at] * collect(grads2, 2 * CX, r, m)

    bins = jnp.zeros((3 * n_tile, LANES), F32)
    for r in range(CX):
        high = (elem[pl.ds(r, 1), :] - first_element) // LANES
        chosen = iota((n_tile, CY), 0) == high
        value = jnp.where(chosen, grad_n[pl.ds(r, 1), :], 0.0)
        bins = bins + lax.dot_general(
            jnp.concatenate(pieces(value), axis=0), one_lo[r], (((1,), (1,)), ((), ())),
            preferred_element_type=F32,
        )
    bins = bins[:n_tile] + bins[n_tile : 2 * n_tile] + bins[2 * n_tile :]
    for k in range(n_tile):
        elem_s[k] = bins[k : k + 1, :]

    def send_bins(step, carry):
        to = lax.rem(t + step, n_tile)
        pltpu.make_async_remote_copy(
            src_ref=elem_s.at[to], dst_ref=elem_r.at[t], send_sem=el_send, recv_sem=el_recv,
            device_id=(g, to), device_id_type=MESH,
        ).start()
        return carry

    lax.fori_loop(1, n_tile, send_bins, 0)
    elem_r[t] = elem_s[t]
    pltpu.make_async_remote_copy(
        src_ref=elem_s.at[everyone], dst_ref=elem_r.at[everyone], send_sem=el_send, recv_sem=el_recv,
        device_id=(g, t), device_id_type=MESH,
    ).wait()
    result = elem_r[0]
    for k in range(1, n_tile):
        result = result + elem_r[k]
    elem_out[...] = result
    leave(moves)
    leave(amoves)


def shards(vel, stress, visc, fric, elem, observed, look, row_owner, row_cell):
    n_grp, n_tile = lax.axis_size("grp"), lax.axis_size("tile")
    rows = observed.shape[0]
    vmem = pl.BlockSpec(memory_space=pltpu.VMEM)
    outgoing = pl.pallas_call(
        functools.partial(rows_kernel, n_grp, n_tile),
        out_shape=jax.ShapeDtypeStruct((n_tile, 8, LANES), F32),
        in_specs=[vmem] * 4,
        out_specs=vmem,
        compiler_params=pltpu.CompilerParams(vmem_limit_bytes=32 << 20),
        name="rows",
    )(look, observed, row_owner.reshape(1, rows), row_cell.reshape(1, rows))
    coefficient = pltpu.VMEM((PICARD, EX, SEG, LANES), F32)
    edge, side = pltpu.VMEM((CX, LANES), F32), pltpu.VMEM((EX, LANES), F32)
    dma = pltpu.SemaphoreType.DMA
    sources = n_grp * n_tile
    stress_adjoint, elements = pl.pallas_call(
        functools.partial(main_kernel, n_grp, n_tile),
        out_shape=(
            jax.ShapeDtypeStruct((2, CX, CY), F32),
            jax.ShapeDtypeStruct((1, LANES), F32),
        ),
        in_specs=[vmem] * 6,
        out_specs=(vmem, vmem),
        scratch_shapes=[
            edge, edge,
            pltpu.VMEM((NF, W, CY), F32), pltpu.VMEM((NF, W, CY), F32),
            side, side,
            pltpu.VMEM((2, CX, CY), F32), pltpu.VMEM((2, W, CY), F32), pltpu.VMEM((2, W, CY), F32),
            edge, edge, side, side,
            pltpu.VMEM((n_tile, 8, LANES), F32),
            pltpu.VMEM((n_grp, n_tile, LANES), F32), pltpu.VMEM((n_grp, n_tile, LANES), F32),
            pltpu.VMEM((15 * CX, SLOTS * sources), BF16), pltpu.VMEM((CY, SLOTS * sources), BF16),
            pltpu.VMEM((5 * CX, CY), F32),
            pltpu.VMEM((NF, EX, SEG, LANES), F32),
            coefficient, coefficient, coefficient, coefficient, coefficient, coefficient,
            pltpu.VMEM((STEPS, 2, CX, SEG, LANES), F32),
            pltpu.VMEM((2, EX, SEG, LANES), F32),
            pltpu.VMEM((3, CX, SEG, LANES), F32),
            pltpu.VMEM((CX, CY), F32),
            pltpu.VMEM((CX, LANES, CY), BF16),
            pltpu.VMEM((n_tile, 1, LANES), F32), pltpu.VMEM((n_tile, 1, LANES), F32),
            dma((14,)), dma((14,)), dma((8,)), dma((8,)),
            dma, dma, dma((n_grp - 1,)), dma((n_grp - 1,)), dma, dma,
        ],
        compiler_params=pltpu.CompilerParams(
            collective_id=0, has_side_effects=True, vmem_limit_bytes=48 << 20
        ),
        name="adjoint",
    )(vel, stress, visc, fric, elem, outgoing)
    return stress_adjoint, elements.reshape(LANES)


def solution(mesh):
    both = ("grp", "tile")
    return jax.shard_map(
        shards,
        mesh=mesh,
        in_specs=(
            P(None, "grp", "tile"),
            P(None, "grp", "tile"),
            P(None, "grp", "tile"),
            P("grp", "tile"),
            P("grp", "tile"),
            P(both, None),
            P(None, both, None),
            P(both, None),
            P(both),
        ),
        out_specs=(P(None, "grp", "tile"), P(both)),
        check_vma=False,
    )
```

time: 1080 us -> 79.6 us (0.07)
  the two profiles are of different devices: /device:TPU:32 before, /device:TPU:1 now
where the time goes in v1:
time: 79.6 us; the launch traced here: 79.4 us
  Pallas kernels  73.8 us (93%)
  local copies, waits for them, and re-layouts  4.81 us (6%)
    pallas_call x1, Pallas kernels, shards(): pl.pallas_call(functools.partial(main_kernel, n_grp, n_tile), out_shape=(...  72.7 us
    unnamed x20, local copies, waits for them, and re-layouts  4.81 us

profile of v1, /device:TPU:1, one launch (start us, length us, event | category | flops | bytes accessed | tf_op | source)
XLA Modules:
  0.0 79.4 jit_solution(14435200554634426376)
XLA Ops:
  0.6 0.0 copy-start.7
  0.6 0.7 copy-done.7
  1.3 0.0 copy-start
  1.3 1.2 %copy-done = f32[2,512,256]{2,1,0:T(8,128)S(1)} copy-done((f32[2,512,256]{2,1,0:T(8,128)S(1)}, f32[2,512,256]{2,1,0:T(8,128)}, u32[]{:S(2)}) %copy-start) | copy-done | bytes 1048600
  2.5 0.0 copy-start.1
  2.5 1.0 %copy-done.1 = f32[512,256]{1,0:T(8,128)S(1)} copy-done((f32[512,256]{1,0:T(8,128)S(1)}, f32[512,256]{1,0:T(8,128)}, u32[]{:S(2)}) %copy-start.1) | copy-done | bytes 524312
  3.6 0.0 copy-start.8
  3.6 0.7 copy-done.8
  4.3 0.0 copy-start.2
  4.3 0.0 copy-start.3
  4.3 0.0 copy-start.4
  4.3 0.0 copy-start.5
  4.3 0.0 copy-start.6
  4.3 1.2 %rows.1.outgoing = f32[32,8,128]{2,1,0:T(8,128)S(1)} custom-call(f32[2,512,256]{2,1,0:T(8,128)S(1)} %copy-done, f32[512,256]{1,0:T(8,128)S(1)} %copy-done.1, s32[1,512]{1,0:T(1,128)S(1)} %bitcast.3, s32[1,512]{1,0:T(1,128)S(1)} %bitcast.4), custom_call_target="tpu_custom_call" | custom-call | tf_op jit(solution)/shard_map/rows/pallas_call | solution.py:468
  5.5 0.0 copy-done.2
  5.5 0.0 copy-done.3
  5.5 0.0 copy-done.4
  5.5 0.0 copy-done.5
  5.5 0.0 copy-done.6
  5.5 72.7 %adjoint.1 = (f32[2,32,512]{2,1,0:T(8,128)S(1)}, f32[1,128]{1,0:T(1,128)S(1)}) custom-call(f32[2,32,512]{2,1,0:T(8,128)S(1)} %copy-done.2, f32[2,32,512]{2,1,0:T(8,128)S(1)} %copy-done.3, f32[2,32,512]{2,1,0:T(8,128)S(1)} %copy-done.4, f32[32,512]{1,0:T(8,128)S(1)} %copy-done.5, s32[32,512]{1,0:T(8,128)S(1)} %copy-done.6, f32[32,8,128]{2,1,0:T(8,128)S(1)} %rows.1.outgoing), custom_call_target="tpu_custom_call" | custom-call | tf_op jit(solution)/shard_map/adjoint/pallas_call | solution.py:480
  78.2 0.7 copy.13
  78.8 0.5 copy.14
Async XLA Ops:
  0.6 0.7 copy-start.7
  1.3 1.2 %copy-start = (f32[2,512,256]{2,1,0:T(8,128)S(1)}, f32[2,512,256]{2,1,0:T(8,128)}, u32[]{:S(2)}) copy-start(f32[2,512,256]{2,1,0:T(8,128)} %look.1) | copy-start | bytes 3145732
  2.5 1.0 %copy-start.1 = (f32[512,256]{1,0:T(8,128)S(1)}, f32[512,256]{1,0:T(8,128)}, u32[]{:S(2)}) copy-start(f32[512,256]{1,0:T(8,128)} %observed.1) | copy-start | bytes 1572868
  3.6 0.7 copy-start.8
  4.3 1.2 %copy-start.2 = (f32[2,32,512]{2,1,0:T(8,128)S(1)}, f32[2,32,512]{2,1,0:T(8,128)}, u32[]{:S(2)}) copy-start(f32[2,32,512]{2,1,0:T(8,128)} %vel.1) | copy-start | bytes 393220
  4.3 1.2 %copy-start.3 = (f32[2,32,512]{2,1,0:T(8,128)S(1)}, f32[2,32,512]{2,1,0:T(8,128)}, u32[]{:S(2)}) copy-start(f32[2,32,512]{2,1,0:T(8,128)} %stress.1) | copy-start | bytes 393220
  4.3 1.2 %copy-start.4 = (f32[2,32,512]{2,1,0:T(8,128)S(1)}, f32[2,32,512]{2,1,0:T(8,128)}, u32[]{:S(2)}) copy-start(f32[2,32,512]{2,1,0:T(8,128)} %visc.1) | copy-start | bytes 393220
  4.3 1.2 %copy-start.5 = (f32[32,512]{1,0:T(8,128)S(1)}, f32[32,512]{1,0:T(8,128)}, u32[]{:S(2)}) copy-start(f32[32,512]{1,0:T(8,128)} %fric.1) | copy-start | bytes 196612
  4.3 1.2 %copy-start.6 = (s32[32,512]{1,0:T(8,128)S(1)}, s32[32,512]{1,0:T(8,128)}, u32[]{:S(2)}) copy-start(s32[32,512]{1,0:T(8,128)} %elem.1) | copy-start | bytes 196612

commit v2 on v1

--- a/solution.py
+++ b/solution.py
@@ -18,8 +18,9 @@
 NF = 7
 SLOTS = 8
 F32, BF16, I32 = jnp.float32, jnp.bfloat16, jnp.int32
-FORWARD = ((0, 4), (4, 4), (8, 4), (12, 4))
-BACKWARD = ((0, 4), (4, 4), (8, 4), (12, 3))
+FORWARD = tuple((start, 2) for start in range(0, STEPS, 2))
+BACKWARD = tuple((start, min(2, STEPS - 1 - start)) for start in range(0, STEPS - 1, 2))
+WHOLE = 34
 
 
 def roll(x, amount):
@@ -45,23 +46,20 @@
     return lax.broadcasted_iota(I32, shape, dim)
 
 
-def rows_kernel(n_grp, n_tile, look, observed, owner, cell, out):
-    rows, epochs = observed.shape
-    devices = n_grp * n_tile
+def row_sums(n_tile, look, observed, owner, cell, out):
+    rows = observed.shape[0]
     owner_row = owner[...]
     lane = iota((rows, LANES), 1)
     owner_col = jnp.transpose(jnp.broadcast_to(owner_row.astype(F32), (LANES, rows)))
     cell_col = jnp.transpose(jnp.broadcast_to(cell[...].astype(F32), (LANES, rows)))
-    mark = owner_col == lane.astype(F32)
-    marks = jnp.where(mark, 1.0, 0.0)
+    marks = jnp.where(owner_col == lane.astype(F32), 1.0, 0.0)
     below = jnp.where(iota((rows, rows), 0) > iota((rows, rows), 1), 1.0, 0.0).astype(BF16)
     before = jnp.dot(below, marks.astype(BF16), preferred_element_type=F32)
     rank = jnp.sum(before * marks, axis=1, keepdims=True)
     x, y, o = look[0], look[1], observed[...]
-    sums = [jnp.sum(a * b, axis=1, keepdims=True) for a, b in ((x, x), (x, y), (y, y), (x, o), (y, o))]
     value = cell_col
-    for j, part in enumerate(sums):
-        value = jnp.where(lane >= SLOTS * (j + 1), part, value)
+    for j, (a, b) in enumerate(((x, x), (x, y), (y, y), (x, o), (y, o))):
+        value = jnp.where(lane >= SLOTS * (j + 1), jnp.sum(a * b, axis=1, keepdims=True), value)
     keep = (rank == (lane % SLOTS).astype(F32)) & (lane < SLOTS * 6)
     value = jnp.where(keep, value, 0.0)
     place = owner_row % n_tile * 8 + owner_row // n_tile
@@ -72,19 +70,26 @@
 
 def main_kernel(
     n_grp, n_tile,
-    vel, stress, visc, fric, elem, outgoing,
+    vel_h, stress_h, visc_h, fric_h, elem_h, observed_h, look_h, owner_h, cell_h,
     stress_out, elem_out,
+    vel, stress, visc, fric, elem, observed, look, owner, cell, outgoing,
     edge_l, edge_r, halo_t, halo_b, halo_l, halo_r,
     adj_n, adj_t, adj_b, aedge_l, aedge_r, ahalo_l, ahalo_r,
     first_r, second_s, second_r, gram_a, gram_b, gram,
     fields, half_q, quart_q, prec, keep_c, drive_u, drive_v,
     moments, adj, grads, grad_n, one_lo, elem_s, elem_r,
-    send_sem, recv_sem, asend_sem, arecv_sem, row_send, row_recv, grp_send, grp_recv, el_send, el_recv,
+    load_sem, send_sem, recv_sem, asend_sem, arecv_sem, row_send, row_recv, grp_send, grp_recv, el_send, el_recv,
 ):
     g, t = lax.axis_index("grp"), lax.axis_index("tile")
     fields2 = fields.reshape(NF * EX * SEG, LANES)
     lane8 = iota((8, LANES), 1)
 
+    pairs = (
+        (vel_h, vel), (stress_h, stress), (visc_h, visc), (fric_h, fric), (owner_h, owner), (cell_h, cell),
+        (look_h, look), (observed_h, observed), (elem_h, elem),
+    )
+    loads = [pltpu.make_async_copy(a, b, load_sem.at[i]) for i, (a, b) in enumerate(pairs)]
+
     barrier = pltpu.get_barrier_semaphore()
     for ref in (halo_t, halo_b, halo_l, halo_r, adj_t, adj_b, ahalo_l, ahalo_r):
         ref[...] = jnp.zeros_like(ref)
@@ -93,19 +98,25 @@
         pl.semaphore_signal(barrier, inc=1, device_id=device, device_id_type=MESH)
 
     up, down, west, east = g > 0, g < n_grp - 1, t > 0, t < n_tile - 1
-    for step in range(1, n_grp):
-        greet((lax.rem(g + step, n_grp), t))
-
-    def greet_tile(step, carry):
-        greet((g, lax.rem(t + step, n_tile)))
-        return carry
-
-    lax.fori_loop(1, n_tile, greet_tile, 0)
     diagonals = ((up & west, -1, -1), (up & east, -1, 1), (down & west, 1, -1), (down & east, 1, 1))
     total = n_grp - 1 + n_tile - 1
     for there, dg, dt in diagonals:
         pl.when(there)(functools.partial(greet, (g + dg, t + dt)))
         total = total + there.astype(I32)
+    greet((g, lax.rem(t + 1, n_tile)))
+    greet((g, lax.rem(t + n_tile - 1, n_tile)))
+    for step in range(1, n_grp):
+        greet((lax.rem(g + step, n_grp), t))
+    for load in loads:
+        load.start()
+
+    def greet_tile(step, carry):
+        greet((g, lax.rem(t + step, n_tile)))
+        return carry
+
+    lax.fori_loop(2, n_tile - 1, greet_tile, 0)
+    for load in loads[:4]:
+        load.wait()
 
     natural = [(vel, 0), (vel, 1), (stress, 0), (stress, 1), (visc, 0), (visc, 1), (fric, None)]
 
@@ -166,14 +177,18 @@
 
     moves = neighbours(
         [
-            (rows_of(vel), halo_t.at[pl.ds(0, 2)], halo_b.at[pl.ds(0, 2)]),
-            (rows_of(stress), halo_t.at[pl.ds(2, 2)], halo_b.at[pl.ds(2, 2)]),
-            (rows_of(visc), halo_t.at[pl.ds(4, 2)], halo_b.at[pl.ds(4, 2)]),
-            (rows_of(fric), halo_t.at[6], halo_b.at[6]),
+            (rows_of(vel_h), halo_t.at[pl.ds(0, 2)], halo_b.at[pl.ds(0, 2)]),
+            (rows_of(stress_h), halo_t.at[pl.ds(2, 2)], halo_b.at[pl.ds(2, 2)]),
+            (rows_of(visc_h), halo_t.at[pl.ds(4, 2)], halo_b.at[pl.ds(4, 2)]),
+            (rows_of(fric_h), halo_t.at[6], halo_b.at[6]),
         ],
         edge_l, edge_r, halo_l, halo_r, send_sem, recv_sem,
     )
     begin(moves)
+
+    for load in loads[4:]:
+        load.wait()
+    row_sums(n_tile, look, observed, owner, cell, outgoing)
 
     def send_rows(step, carry):
         to = lax.rem(t + step, n_tile)
@@ -245,35 +260,44 @@
                 drive_v[p, k] = c * fields[3, k]
             q_old = q
 
-    def stencil(load, p, lo, hi, use):
-        prev, stress_prev = None, None
-        for k in range(lo - 1, hi + 2):
+    def stencil(load, p, lo, count, use):
+        def node(k):
             a, b = load(k)
             la, lb = right(a), right(b)
-            xa, yb = a + la, lb - b
-            ya, xb = la - a, b + lb
-            plus, minus = ya + xb, ya - xb
-            now = None
-            if prev is not None:
-                xm = xa - prev[0]
-                ym = yb + prev[1]
-                sh = plus + prev[2]
-                both = xm + ym
-                h = half_q[p, k - 1]
-                now = (h * (both + xm), h * (both + ym), quart_q[p, k - 1] * sh)
-                if stress_prev is not None:
-                    dxx = stress_prev[0] - now[0]
-                    myy = stress_prev[1] + now[1]
-                    mxy = stress_prev[2] + now[2]
-                    dxy = stress_prev[2] - now[2]
-                    use(k - 1, (dxx - mxy) + left(dxx + mxy), (dxy - myy) + left(dxy + myy), prev[3], prev[4])
-            prev, stress_prev = (xa, yb, minus, a, b), now
+            xa, yb, ya, xb = a + la, lb - b, la - a, b + lb
+            return xa, yb, ya + xb, ya - xb, a, b
+
+        def quad(k, old, new):
+            xm, ym, sh = new[0] - old[0], new[1] + old[1], new[2] + old[3]
+            both = xm + ym
+            h = half_q[p, k]
+            return h * (both + xm), h * (both + ym), quart_q[p, k] * sh
+
+        def run(base, rows, carry):
+            here, above = carry
+            for r in range(rows):
+                k = base + r
+                after = node(k + 1)
+                below = quad(k, here, after)
+                dxx, myy = above[0] - below[0], above[1] + below[1]
+                mxy, dxy = above[2] + below[2], above[2] - below[2]
+                use(k, (dxx - mxy) + left(dxx + mxy), (dxy - myy) + left(dxy + myy), here[4], here[5])
+                here, above = after, below
+            return here, above
+
+        before = node(lo - 1)
+        here = node(lo)
+        carry = (here, quad(lo - 1, before, here))
+        if count <= WHOLE:
+            run(lo, count, carry)
+        else:
+            rows = count // 2
+            lax.fori_loop(0, 2, lambda i, carry: run(lo + i * rows, rows, carry), carry)
 
     inv = 1.0 / 0.45
 
     def forward(start, count):
         p = start // SWEEPS
-        lo, hi = start + 1, EX - 2 - start
 
         def sweep(s, carry):
             def use(k, first, second, u, v):
@@ -282,16 +306,15 @@
                 new_v = (d * v + drive_v[p, k]) - c * second
                 fields[0, k] = new_u
                 fields[1, k] = new_v
-                if W <= k < W + CX:
-                    moments[s, 0, k - W] = inv * new_u + (1.0 - inv) * u
-                    moments[s, 1, k - W] = inv * new_v + (1.0 - inv) * v
-
-            stencil(lambda k: (fields[0, k], fields[1, k]), p, lo, hi, use)
+                moments[s, 0, k] = inv * new_u + (1.0 - inv) * u
+                moments[s, 1, k] = inv * new_v + (1.0 - inv) * v
+
+            stencil(lambda k: (fields[0, k], fields[1, k]), p, start + 1, EX - 2 - 2 * start, use)
             return carry
 
         lax.fori_loop(start, start + count, sweep, 0)
 
-    for start, count in FORWARD[:2]:
+    for start, count in FORWARD[:4]:
         forward(start, count)
 
     everyone = pl.ds(0, n_tile - 1)
@@ -316,7 +339,8 @@
     for step in range(1, n_grp):
         group_copy(step).start()
 
-    forward(*FORWARD[2])
+    for start, count in FORWARD[4:6]:
+        forward(start, count)
 
     for step in range(1, n_grp):
         group_copy(step).wait()
@@ -338,7 +362,8 @@
     part = 5 * CX
     gram[...] = product[:part] + product[part : 2 * part] + product[2 * part :]
 
-    forward(*FORWARD[3])
+    for start, count in FORWARD[6:]:
+        forward(start, count)
 
     def collect(source, base, r, m):
         a = source[pl.ds(base * SEG + 8 * SEG * r + 2 * m, 8, stride=SEG), :]
@@ -385,21 +410,18 @@
             )
 
     def gather(position, k, a, b):
-        i = k - W
-        grads[0, i] = grads[0, i] + a
-        grads[1, i] = grads[1, i] + b
-        grads[2, i] = grads[2, i] - (a * moments[position, 0, i] + b * moments[position, 1, i])
+        grads[0, k] = grads[0, k] + a
+        grads[1, k] = grads[1, k] + b
+        grads[2, k] = grads[2, k] - (a * moments[position, 0, k] + b * moments[position, 1, k])
 
     def backward(start, count):
         p = (STEPS - 1 - start) // SWEEPS
-        lo, hi = start + 2, EX - 3 - start
 
         def sweep(s, carry):
             def load(k):
                 c = prec[p, k]
                 a, b = c * adj[0, k], c * adj[1, k]
-                if W <= k < W + CX:
-                    gather(STEPS - 1 - s, k, a, b)
+                gather(STEPS - 1 - s, k, a, b)
                 return a, b
 
             def use(k, first, second, a, b):
@@ -407,7 +429,7 @@
                 adj[0, k] = d * adj[0, k] - first
                 adj[1, k] = d * adj[1, k] - second
 
-            stencil(load, p, lo, hi, use)
+            stencil(load, p, start + 2, EX - 4 - 2 * start, use)
             return carry
 
         lax.fori_loop(start, start + count, sweep, 0)
@@ -418,13 +440,13 @@
         c = prec[0, k]
         gather(0, k, c * adj[0, k], c * adj[1, k])
 
-    grads2 = grads.reshape(3 * CX * SEG, LANES)
+    grads2 = grads.reshape(3 * EX * SEG, LANES)
     for r in range(CX // 8):
         for m in range(CY // LANES):
             rows, at = pl.ds(8 * r, 8), pl.ds(LANES * m, LANES)
-            stress_out[0, rows, at] = collect(grads2, 0, r, m)
-            stress_out[1, rows, at] = collect(grads2, CX, r, m)
-            grad_n[rows, at] = fric[rows, at] * collect(grads2, 2 * CX, r, m)
+            stress_out[0, rows, at] = collect(grads2, W, r, m)
+            stress_out[1, rows, at] = collect(grads2, EX + W, r, m)
+            grad_n[rows, at] = fric[rows, at] * collect(grads2, 2 * EX + W, r, m)
 
     bins = jnp.zeros((3 * n_tile, LANES), F32)
     for r in range(CX):
@@ -465,14 +487,7 @@
     n_grp, n_tile = lax.axis_size("grp"), lax.axis_size("tile")
     rows = observed.shape[0]
     vmem = pl.BlockSpec(memory_space=pltpu.VMEM)
-    outgoing = pl.pallas_call(
-        functools.partial(rows_kernel, n_grp, n_tile),
-        out_shape=jax.ShapeDtypeStruct((n_tile, 8, LANES), F32),
-        in_specs=[vmem] * 4,
-        out_specs=vmem,
-        compiler_params=pltpu.CompilerParams(vmem_limit_bytes=32 << 20),
-        name="rows",
-    )(look, observed, row_owner.reshape(1, rows), row_cell.reshape(1, rows))
+    hbm = pl.BlockSpec(memory_space=pltpu.HBM)
     coefficient = pltpu.VMEM((PICARD, EX, SEG, LANES), F32)
     edge, side = pltpu.VMEM((CX, LANES), F32), pltpu.VMEM((EX, LANES), F32)
     dma = pltpu.SemaphoreType.DMA
@@ -483,9 +498,14 @@
             jax.ShapeDtypeStruct((2, CX, CY), F32),
             jax.ShapeDtypeStruct((1, LANES), F32),
         ),
-        in_specs=[vmem] * 6,
+        in_specs=[hbm] * 9,
         out_specs=(vmem, vmem),
         scratch_shapes=[
+            pltpu.VMEM((2, CX, CY), F32), pltpu.VMEM((2, CX, CY), F32), pltpu.VMEM((2, CX, CY), F32),
+            pltpu.VMEM((CX, CY), F32), pltpu.VMEM((CX, CY), I32),
+            pltpu.VMEM(observed.shape, F32), pltpu.VMEM(look.shape, F32),
+            pltpu.VMEM((1, rows), I32), pltpu.VMEM((1, rows), I32),
+            pltpu.VMEM((n_tile, 8, LANES), F32),
             edge, edge,
             pltpu.VMEM((NF, W, CY), F32), pltpu.VMEM((NF, W, CY), F32),
             side, side,
@@ -497,20 +517,23 @@
             pltpu.VMEM((5 * CX, CY), F32),
             pltpu.VMEM((NF, EX, SEG, LANES), F32),
             coefficient, coefficient, coefficient, coefficient, coefficient, coefficient,
-            pltpu.VMEM((STEPS, 2, CX, SEG, LANES), F32),
+            pltpu.VMEM((STEPS, 2, EX, SEG, LANES), F32),
             pltpu.VMEM((2, EX, SEG, LANES), F32),
-            pltpu.VMEM((3, CX, SEG, LANES), F32),
+            pltpu.VMEM((3, EX, SEG, LANES), F32),
             pltpu.VMEM((CX, CY), F32),
             pltpu.VMEM((CX, LANES, CY), BF16),
             pltpu.VMEM((n_tile, 1, LANES), F32), pltpu.VMEM((n_tile, 1, LANES), F32),
-            dma((14,)), dma((14,)), dma((8,)), dma((8,)),
+            dma((9,)), dma((14,)), dma((14,)), dma((8,)), dma((8,)),
             dma, dma, dma((n_grp - 1,)), dma((n_grp - 1,)), dma, dma,
         ],
         compiler_params=pltpu.CompilerParams(
-            collective_id=0, has_side_effects=True, vmem_limit_bytes=48 << 20
+            collective_id=0, has_side_effects=True, vmem_limit_bytes=56 << 20
         ),
         name="adjoint",
-    )(vel, stress, visc, fric, elem, outgoing)
+    )(
+        vel, stress, visc, fric, elem, observed, look,
+        row_owner.reshape(1, rows), row_cell.reshape(1, rows),
+    )
     return stress_adjoint, elements.reshape(LANES)
 
 

time: 79.6 us -> 52.7 us (0.66)
  Pallas kernels: 73.8 us -> 49.8 us
  local copies, waits for them, and re-layouts: 4.81 us -> 2.08 us
    pallas_call x1, Pallas kernels: 72.7 us -> 49.8 us  [shards(): pl.pallas_call(functools.partial(main_kernel, n_grp, n_tile), out_shape=(...]
    unnamed x20 -> x4, local copies, waits for them, and re-layouts: 4.81 us -> 2.08 us
    pallas_call x1 -> x0, Pallas kernels: 1.16 us -> none  [shards(): pl.pallas_call(functools.partial(rows_kernel, n_grp, n_tile), out_shape=j...]
where the time goes in v2:
time: 52.7 us; the launch traced here: 52.5 us
  Pallas kernels  49.8 us (94%)
  local copies, waits for them, and re-layouts  2.08 us (4%)
  between operations  0.65 us (1%)
    pallas_call x1, Pallas kernels, shards(): pl.pallas_call(functools.partial(main_kernel, n_grp, n_tile), out_shape=(...  49.8 us
    unnamed x4, local copies, waits for them, and re-layouts  2.08 us

profile of v2, /device:TPU:1, one launch (start us, length us, event | category | flops | bytes accessed | tf_op | source)
XLA Modules:
  0.0 52.5 jit_solution(18292445566819775770)
XLA Ops:
  0.6 49.8 %adjoint.1 = (f32[2,32,512]{2,1,0:T(8,128)}, f32[1,128]{1,0:T(1,128)}) custom-call(f32[2,32,512]{2,1,0:T(8,128)} %vel_h.1, f32[2,32,512]{2,1,0:T(8,128)} %stress_h.1, f32[2,32,512]{2,1,0:T(8,128)} %visc_h.1, f32[32,512]{1,0:T(8,128)} %fric_h.1, s32[32,512]{1,0:T(8,128)} %elem_h.1, f32[512,256]{1,0:T(8,128)} %observed_h.1, f32[2,512,256]{2,1,0:T(8,128)} %look_h.1, ...), custom_call_target="tpu_custom_call" | custom-call | tf_op jit(solution)/shard_map/adjoint/pallas_call | solution.py:495
  50.4 0.0 copy-start
  50.5 1.6 %copy.13 = f32[2,32,512]{2,1,0:T(8,128)} copy(f32[2,32,512]{2,1,0:T(8,128)} %get-tuple-element.8) | data formatting | bytes 262144
  52.0 0.0 copy-done
  52.0 0.5 copy.14
Async XLA Ops:
  50.4 1.6 %copy-start = (f32[1,128]{1,0:T(1,128)S(1)}, f32[1,128]{1,0:T(1,128)}, u32[]{:S(2)}) copy-start(f32[1,128]{1,0:T(1,128)} %get-tuple-element.5) | copy-start | bytes 1540

commit v3 on v2

--- a/solution.py
+++ b/solution.py
@@ -135,13 +135,13 @@
         edge_l[pl.ds(8 * r, 8), :] = low
         edge_r[pl.ds(8 * r, 8), :] = high
 
+    for load in loads[4:]:
+        load.wait()
+    row_sums(n_tile, look, observed, owner, cell, outgoing)
     pl.semaphore_wait(barrier, total)
 
     def neighbours(blocks, e_l, e_r, h_l, h_r, send, recv):
         moves = []
-        for ref, h_t, h_b in blocks:
-            moves.append((down, up, ref(W), h_t, (g + 1, t)))
-            moves.append((up, down, ref(0), h_b, (g - 1, t)))
         moves.append((east, west, e_r, h_l.at[pl.ds(W, CX)], (g, t + 1)))
         moves.append((west, east, e_l, h_r.at[pl.ds(W, CX)], (g, t - 1)))
         last, head, foot = pl.ds(W, W), pl.ds(0, W), pl.ds(W + CX, W)
@@ -149,6 +149,9 @@
         moves.append((up & east, down & west, e_r.at[head], h_l.at[foot], (g - 1, t + 1)))
         moves.append((down & west, up & east, e_l.at[last], h_r.at[head], (g + 1, t - 1)))
         moves.append((up & west, down & east, e_l.at[head], h_r.at[foot], (g - 1, t - 1)))
+        for ref, h_t, h_b in blocks:
+            moves.append((down, up, ref(W), h_t, (g + 1, t)))
+            moves.append((up, down, ref(0), h_b, (g - 1, t)))
         out = []
         for i, (sends, gets, source, target, device) in enumerate(moves):
             copy = pltpu.make_async_remote_copy(
@@ -185,10 +188,6 @@
         edge_l, edge_r, halo_l, halo_r, send_sem, recv_sem,
     )
     begin(moves)
-
-    for load in loads[4:]:
-        load.wait()
-    row_sums(n_tile, look, observed, owner, cell, outgoing)
 
     def send_rows(step, carry):
         to = lax.rem(t + step, n_tile)
@@ -314,7 +313,7 @@
 
         lax.fori_loop(start, start + count, sweep, 0)
 
-    for start, count in FORWARD[:4]:
+    for start, count in FORWARD[:2]:
         forward(start, count)
 
     everyone = pl.ds(0, n_tile - 1)
@@ -339,7 +338,7 @@
     for step in range(1, n_grp):
         group_copy(step).start()
 
-    for start, count in FORWARD[4:6]:
+    for start, count in FORWARD[2:6]:
         forward(start, count)
 
     for step in range(1, n_grp):
@@ -347,10 +346,10 @@
     sources = n_grp * n_tile
     arrived = jnp.transpose(second_r[...].reshape(sources, LANES))
     for s in range(SLOTS):
-        cell = arrived[s : s + 1, :].astype(I32)
+        spot = arrived[s : s + 1, :].astype(I32)
         at = pl.ds(s * sources, sources)
-        gram_b[:, at] = jnp.where(iota((CY, sources), 0) == cell % CY, 1.0, 0.0).astype(BF16)
-        chosen = iota((CX, sources), 0) == cell // CY
+        gram_b[:, at] = jnp.where(iota((CY, sources), 0) == spot % CY, 1.0, 0.0).astype(BF16)
+        chosen = iota((CX, sources), 0) == spot // CY
         for j in range(5):
             row = SLOTS * (j + 1) + s
             value = jnp.where(chosen, arrived[row : row + 1, :], 0.0)
@@ -444,8 +443,6 @@
     for r in range(CX // 8):
         for m in range(CY // LANES):
             rows, at = pl.ds(8 * r, 8), pl.ds(LANES * m, LANES)
-            stress_out[0, rows, at] = collect(grads2, W, r, m)
-            stress_out[1, rows, at] = collect(grads2, EX + W, r, m)
             grad_n[rows, at] = fric[rows, at] * collect(grads2, 2 * EX + W, r, m)
 
     bins = jnp.zeros((3 * n_tile, LANES), F32)
@@ -471,6 +468,11 @@
 
     lax.fori_loop(1, n_tile, send_bins, 0)
     elem_r[t] = elem_s[t]
+    for r in range(CX // 8):
+        for m in range(CY // LANES):
+            rows, at = pl.ds(8 * r, 8), pl.ds(LANES * m, LANES)
+            stress_out[0, rows, at] = collect(grads2, W, r, m)
+            stress_out[1, rows, at] = collect(grads2, EX + W, r, m)
     pltpu.make_async_remote_copy(
         src_ref=elem_s.at[everyone], dst_ref=elem_r.at[everyone], send_sem=el_send, recv_sem=el_recv,
         device_id=(g, t), device_id_type=MESH,
@@ -478,7 +480,7 @@
     result = elem_r[0]
     for k in range(1, n_tile):
         result = result + elem_r[k]
-    elem_out[...] = result
+    elem_out[...] = result.reshape(LANES)
     leave(moves)
     leave(amoves)
 
@@ -496,7 +498,7 @@
         functools.partial(main_kernel, n_grp, n_tile),
         out_shape=(
             jax.ShapeDtypeStruct((2, CX, CY), F32),
-            jax.ShapeDtypeStruct((1, LANES), F32),
+            jax.ShapeDtypeStruct((LANES,), F32),
         ),
         in_specs=[hbm] * 9,
         out_specs=(vmem, vmem),
@@ -534,7 +536,7 @@
         vel, stress, visc, fric, elem, observed, look,
         row_owner.reshape(1, rows), row_cell.reshape(1, rows),
     )
-    return stress_adjoint, elements.reshape(LANES)
+    return stress_adjoint, elements
 
 
 def solution(mesh):

time: 52.7 us -> 51.3 us (0.973)
  Pallas kernels: 49.8 us -> 48.4 us
    pallas_call x1, Pallas kernels: 49.8 us -> 48.4 us  [shards(): pl.pallas_call(functools.partial(main_kernel, n_grp, n_tile), out_shape=(...]
where the time goes in v3:
time: 51.3 us; the launch traced here: 51.1 us
  Pallas kernels  48.4 us (94%)
  local copies, waits for them, and re-layouts  2.08 us (4%)
  between operations  0.65 us (1%)
    pallas_call x1, Pallas kernels, shards(): pl.pallas_call(functools.partial(main_kernel, n_grp, n_tile), out_shape=(...  48.4 us
    unnamed x4, local copies, waits for them, and re-layouts  2.08 us

profile of v3, /device:TPU:1, one launch (start us, length us, event | category | flops | bytes accessed | tf_op | source)
XLA Modules:
  0.0 51.1 jit_solution(13656337772677429042)
XLA Ops:
  0.6 48.4 %adjoint.1 = (f32[2,32,512]{2,1,0:T(8,128)}, f32[128]{0:T(128)}) custom-call(f32[2,32,512]{2,1,0:T(8,128)} %vel_h.1, f32[2,32,512]{2,1,0:T(8,128)} %stress_h.1, f32[2,32,512]{2,1,0:T(8,128)} %visc_h.1, f32[32,512]{1,0:T(8,128)} %fric_h.1, s32[32,512]{1,0:T(8,128)} %elem_h.1, f32[512,256]{1,0:T(8,128)} %observed_h.1, f32[2,512,256]{2,1,0:T(8,128)} %look_h.1, ...), custom_call_target="tpu_custom_call" | custom-call | tf_op jit(solution)/shard_map/adjoint/pallas_call | solution.py:497
  49.0 0.0 copy-start
  49.0 1.6 %copy.13 = f32[2,32,512]{2,1,0:T(8,128)} copy(f32[2,32,512]{2,1,0:T(8,128)} %get-tuple-element.4) | data formatting | bytes 262144
  50.6 0.0 copy-done
  50.6 0.5 %copy.14 = f32[128]{0:T(128)} copy(f32[128]{0:T(128)S(1)} %copy-done) | data formatting | bytes 1024
Async XLA Ops:
  49.0 1.6 %copy-start = (f32[128]{0:T(128)S(1)}, f32[128]{0:T(128)}, u32[]{:S(2)}) copy-start(f32[128]{0:T(128)} %get-tuple-element.5) | copy-start | bytes 1540

commit v4 on v3

--- a/solution.py
+++ b/solution.py
@@ -18,8 +18,12 @@
 NF = 7
 SLOTS = 8
 F32, BF16, I32 = jnp.float32, jnp.bfloat16, jnp.int32
-FORWARD = tuple((start, 2) for start in range(0, STEPS, 2))
-BACKWARD = tuple((start, min(2, STEPS - 1 - start)) for start in range(0, STEPS - 1, 2))
+FORWARD = tuple((start, 1) for start in range(STEPS - 2)) + ((STEPS - 2, 2),)
+BACKWARD = tuple((start, 1) for start in range(STEPS - 3)) + ((STEPS - 3, 2),)
+HOPS = sorted(
+    [(x, y, z) for x in range(4) for y in range(4) for z in range(2) if x + y + z],
+    key=lambda d: -(min(d[0], 4 - d[0]) + min(d[1], 4 - d[1]) + 2 * d[2]),
+)
 WHOLE = 34
 
 
@@ -94,27 +98,26 @@
     for ref in (halo_t, halo_b, halo_l, halo_r, adj_t, adj_b, ahalo_l, ahalo_r):
         ref[...] = jnp.zeros_like(ref)
 
+    def partner(hop):
+        x, y, z = hop
+        return (t // 8 + x) % 4 * 8 + (t // 2 + y) % 4 * 2 + (t + z) % 2
+
     def greet(device):
         pl.semaphore_signal(barrier, inc=1, device_id=device, device_id_type=MESH)
 
     up, down, west, east = g > 0, g < n_grp - 1, t > 0, t < n_tile - 1
     diagonals = ((up & west, -1, -1), (up & east, -1, 1), (down & west, 1, -1), (down & east, 1, 1))
     total = n_grp - 1 + n_tile - 1
+    for hop in HOPS:
+        greet((g, partner(hop)))
     for there, dg, dt in diagonals:
         pl.when(there)(functools.partial(greet, (g + dg, t + dt)))
         total = total + there.astype(I32)
-    greet((g, lax.rem(t + 1, n_tile)))
-    greet((g, lax.rem(t + n_tile - 1, n_tile)))
     for step in range(1, n_grp):
         greet((lax.rem(g + step, n_grp), t))
     for load in loads:
         load.start()
 
-    def greet_tile(step, carry):
-        greet((g, lax.rem(t + step, n_tile)))
-        return carry
-
-    lax.fori_loop(2, n_tile - 1, greet_tile, 0)
     for load in loads[:4]:
         load.wait()
 
@@ -180,46 +183,49 @@
 
     moves = neighbours(
         [
-            (rows_of(vel_h), halo_t.at[pl.ds(0, 2)], halo_b.at[pl.ds(0, 2)]),
-            (rows_of(stress_h), halo_t.at[pl.ds(2, 2)], halo_b.at[pl.ds(2, 2)]),
-            (rows_of(visc_h), halo_t.at[pl.ds(4, 2)], halo_b.at[pl.ds(4, 2)]),
-            (rows_of(fric_h), halo_t.at[6], halo_b.at[6]),
+            (rows_of(vel), halo_t.at[pl.ds(0, 2)], halo_b.at[pl.ds(0, 2)]),
+            (rows_of(stress), halo_t.at[pl.ds(2, 2)], halo_b.at[pl.ds(2, 2)]),
+            (rows_of(visc), halo_t.at[pl.ds(4, 2)], halo_b.at[pl.ds(4, 2)]),
+            (rows_of(fric), halo_t.at[6], halo_b.at[6]),
         ],
         edge_l, edge_r, halo_l, halo_r, send_sem, recv_sem,
     )
     begin(moves)
 
-    def send_rows(step, carry):
-        to = lax.rem(t + step, n_tile)
+    for hop in HOPS:
+        to = partner(hop)
         pltpu.make_async_remote_copy(
-            src_ref=outgoing.at[to], dst_ref=first_r.at[t], send_sem=row_send, recv_sem=row_recv,
+            src_ref=outgoing.at[to, pl.ds(0, n_grp)], dst_ref=first_r.at[t, pl.ds(0, n_grp)], send_sem=row_send, recv_sem=row_recv,
             device_id=(g, to), device_id_type=MESH,
         ).start()
-        return carry
-
-    lax.fori_loop(1, n_tile, send_rows, 0)
 
     first_element = g * (n_tile * LANES)
     for r in range(CX):
         low = (elem[pl.ds(r, 1), :] - first_element) % LANES
         one_lo[r] = jnp.where(iota((LANES, CY), 0) == low, 1.0, 0.0).astype(BF16)
 
-    def spread(target, base, row, tiles, before, after):
+    def spread(target, base, row, tiles, before, after, inner=True, outer=True):
         wide = [roll(x, 32) for x in tiles]
         back = [roll(x, -32) for x in tiles]
         for m in range(CY // LANES):
             even = jnp.where(lane8 < 32, before if m == 0 else wide[m - 1], wide[m])
             odd = jnp.where(lane8 < 96, back[m], after if m == CY // LANES - 1 else back[m + 1])
-            target[pl.ds((base + row) * SEG + 2 * m, 8, stride=SEG), :] = even
-            target[pl.ds((base + row) * SEG + 2 * m + 1, 8, stride=SEG), :] = odd
-
-    def spread_block(f, r, tiles):
+            if outer if m == 0 else inner:
+                target[pl.ds((base + row) * SEG + 2 * m, 8, stride=SEG), :] = even
+            if outer if m == CY // LANES - 1 else inner:
+                target[pl.ds((base + row) * SEG + 2 * m + 1, 8, stride=SEG), :] = odd
+
+    def spread_block(f, r, tiles, inner):
         at = pl.ds(8 * r, 8)
         spread(
             fields2, f * EX, 8 * r, tiles,
-            roll(halo_l[at, :], 16 - 16 * f), roll(halo_r[at, :], 96 - 16 * f),
+            roll(halo_l[at, :], 16 - 16 * f), roll(halo_r[at, :], 96 - 16 * f), inner=inner,
         )
 
+    for f in range(NF):
+        for r in range(CX // 8):
+            tiles = [tile_of(f, r, m) for m in range(4)]
+            spread(fields2, f * EX, W + 8 * r, tiles, tiles[0], tiles[-1], outer=False)
     arrive(moves)
     for f in range(NF):
         for r in range(EX // 8):
@@ -230,7 +236,7 @@
                 tiles = [halo_b[f, pl.ds(8 * k, 8), pl.ds(LANES * m, LANES)] for m in range(4)]
             else:
                 tiles = [tile_of(f, r - W // 8, m) for m in range(4)]
-            spread_block(f, r, tiles)
+            spread_block(f, r, tiles, not W // 8 <= r < (W + CX) // 8)
 
     seg8 = iota((SEG, LANES), 0)
     inside = ((t > 0) | (seg8 > 0) | (lane8 >= 32)) & ((t < n_tile - 1) | (seg8 < SEG - 1) | (lane8 < 96))
@@ -313,12 +319,12 @@
 
         lax.fori_loop(start, start + count, sweep, 0)
 
-    for start, count in FORWARD[:2]:
+    for start, count in FORWARD[:4]:
         forward(start, count)
 
     everyone = pl.ds(0, n_tile - 1)
     pltpu.make_async_remote_copy(
-        src_ref=outgoing.at[everyone], dst_ref=first_r.at[everyone], send_sem=row_send, recv_sem=row_recv,
+        src_ref=outgoing.at[everyone, pl.ds(0, n_grp)], dst_ref=first_r.at[everyone, pl.ds(0, n_grp)], send_sem=row_send, recv_sem=row_recv,
         device_id=(g, t), device_id_type=MESH,
     ).wait()
     own = outgoing[t]
@@ -338,7 +344,7 @@
     for step in range(1, n_grp):
         group_copy(step).start()
 
-    for start, count in FORWARD[2:6]:
+    for start, count in FORWARD[4:12]:
         forward(start, count)
 
     for step in range(1, n_grp):
@@ -361,7 +367,7 @@
     part = 5 * CX
     gram[...] = product[:part] + product[part : 2 * part] + product[2 * part :]
 
-    for start, count in FORWARD[6:]:
+    for start, count in FORWARD[12:]:
         forward(start, count)
 
     def collect(source, base, r, m):
@@ -458,15 +464,12 @@
     for k in range(n_tile):
         elem_s[k] = bins[k : k + 1, :]
 
-    def send_bins(step, carry):
-        to = lax.rem(t + step, n_tile)
+    for hop in HOPS:
+        to = partner(hop)
         pltpu.make_async_remote_copy(
             src_ref=elem_s.at[to], dst_ref=elem_r.at[t], send_sem=el_send, recv_sem=el_recv,
             device_id=(g, to), device_id_type=MESH,
         ).start()
-        return carry
-
-    lax.fori_loop(1, n_tile, send_bins, 0)
     elem_r[t] = elem_s[t]
     for r in range(CX // 8):
         for m in range(CY // LANES):

time: 51.3 us -> 50.1 us (0.977)
  Pallas kernels: 48.4 us -> 47.2 us
    pallas_call x1, Pallas kernels: 48.4 us -> 47.2 us  [shards(): pl.pallas_call(functools.partial(main_kernel, n_grp, n_tile), out_shape=(...]
where the time goes in v4:
time: 50.1 us; the launch traced here: 50 us
  Pallas kernels  47.2 us (94%)
  local copies, waits for them, and re-layouts  2.08 us (4%)
  between operations  0.65 us (1%)
    pallas_call x1, Pallas kernels, shards(): pl.pallas_call(functools.partial(main_kernel, n_grp, n_tile), out_shape=(...  47.2 us
    unnamed x4, local copies, waits for them, and re-layouts  2.08 us

profile of v4, /device:TPU:1, one launch (start us, length us, event | category | flops | bytes accessed | tf_op | source)
XLA Modules:
  0.0 50.0 jit_solution(2835386171549622972)
XLA Ops:
  0.6 47.2 %adjoint.1 = (f32[2,32,512]{2,1,0:T(8,128)}, f32[128]{0:T(128)}) custom-call(f32[2,32,512]{2,1,0:T(8,128)} %vel_h.1, f32[2,32,512]{2,1,0:T(8,128)} %stress_h.1, f32[2,32,512]{2,1,0:T(8,128)} %visc_h.1, f32[32,512]{1,0:T(8,128)} %fric_h.1, s32[32,512]{1,0:T(8,128)} %elem_h.1, f32[512,256]{1,0:T(8,128)} %observed_h.1, f32[2,512,256]{2,1,0:T(8,128)} %look_h.1, ...), custom_call_target="tpu_custom_call" | custom-call | tf_op jit(solution)/shard_map/adjoint/pallas_call | solution.py:500
  47.9 0.0 copy-start
  47.9 1.6 %copy.13 = f32[2,32,512]{2,1,0:T(8,128)} copy(f32[2,32,512]{2,1,0:T(8,128)} %get-tuple-element.4) | data formatting | bytes 262144
  49.4 0.0 copy-done
  49.5 0.5 %copy.14 = f32[128]{0:T(128)} copy(f32[128]{0:T(128)S(1)} %copy-done) | data formatting | bytes 1024
Async XLA Ops:
  47.9 1.6 %copy-start = (f32[128]{0:T(128)S(1)}, f32[128]{0:T(128)}, u32[]{:S(2)}) copy-start(f32[128]{0:T(128)} %get-tuple-element.5) | copy-start | bytes 1540

commit v5 on v4

--- a/solution.py
+++ b/solution.py
@@ -185,12 +185,14 @@
         [
             (rows_of(vel), halo_t.at[pl.ds(0, 2)], halo_b.at[pl.ds(0, 2)]),
             (rows_of(stress), halo_t.at[pl.ds(2, 2)], halo_b.at[pl.ds(2, 2)]),
-            (rows_of(visc), halo_t.at[pl.ds(4, 2)], halo_b.at[pl.ds(4, 2)]),
+            (rows_of(visc.at[0]), halo_t.at[4], halo_b.at[4]),
             (rows_of(fric), halo_t.at[6], halo_b.at[6]),
+            (rows_of(visc.at[1]), halo_t.at[5], halo_b.at[5]),
         ],
         edge_l, edge_r, halo_l, halo_r, send_sem, recv_sem,
     )
     begin(moves)
+    moves, late = moves[:-2], moves[-2:]
 
     for hop in HOPS:
         to = partner(hop)
@@ -226,23 +228,27 @@
         for r in range(CX // 8):
             tiles = [tile_of(f, r, m) for m in range(4)]
             spread(fields2, f * EX, W + 8 * r, tiles, tiles[0], tiles[-1], outer=False)
-    arrive(moves)
-    for f in range(NF):
+    def settle(f):
         for r in range(EX // 8):
+            inner = not W // 8 <= r < (W + CX) // 8
             if r < W // 8:
                 tiles = [halo_t[f, pl.ds(8 * r, 8), pl.ds(LANES * m, LANES)] for m in range(4)]
-            elif r >= (W + CX) // 8:
+            elif inner:
                 k = r - (W + CX) // 8
                 tiles = [halo_b[f, pl.ds(8 * k, 8), pl.ds(LANES * m, LANES)] for m in range(4)]
             else:
                 tiles = [tile_of(f, r - W // 8, m) for m in range(4)]
-            spread_block(f, r, tiles, not W // 8 <= r < (W + CX) // 8)
+            spread_block(f, r, tiles, inner)
+
+    arrive(moves)
+    for f in (0, 1, 2, 3, 4, 6):
+        settle(f)
 
     seg8 = iota((SEG, LANES), 0)
     inside = ((t > 0) | (seg8 > 0) | (lane8 >= 32)) & ((t < n_tile - 1) | (seg8 < SEG - 1) | (lane8 < 96))
     inside_top = inside & up
     inside_bottom = inside & down
-    for p in range(PICARD):
+    def coefficients(p):
         pair = fields[4 + p, 0]
         pair = pair + right(pair)
         q_old = None
@@ -265,6 +271,8 @@
                 drive_v[p, k] = c * fields[3, k]
             q_old = q
 
+    coefficients(0)
+
     def stencil(load, p, lo, count, use):
         def node(k):
             a, b = load(k)
@@ -344,7 +352,12 @@
     for step in range(1, n_grp):
         group_copy(step).start()
 
-    for start, count in FORWARD[4:12]:
+    for start, count in FORWARD[4:SWEEPS]:
+        forward(start, count)
+    arrive(late)
+    settle(5)
+    coefficients(1)
+    for start, count in FORWARD[SWEEPS:12]:
         forward(start, count)
 
     for step in range(1, n_grp):
@@ -485,6 +498,7 @@
         result = result + elem_r[k]
     elem_out[...] = result.reshape(LANES)
     leave(moves)
+    leave(late)
     leave(amoves)
 
 
@@ -528,7 +542,7 @@
             pltpu.VMEM((CX, CY), F32),
             pltpu.VMEM((CX, LANES, CY), BF16),
             pltpu.VMEM((n_tile, 1, LANES), F32), pltpu.VMEM((n_tile, 1, LANES), F32),
-            dma((9,)), dma((14,)), dma((14,)), dma((8,)), dma((8,)),
+            dma((9,)), dma((16,)), dma((16,)), dma((8,)), dma((8,)),
             dma, dma, dma((n_grp - 1,)), dma((n_grp - 1,)), dma, dma,
         ],
         compiler_params=pltpu.CompilerParams(

time: 50.1 us -> 49.8 us (level)
  no operation moved by 1% of the time
where the time goes in v5:
time: 49.8 us; the launch traced here: 49.7 us
  Pallas kernels  46.9 us (94%)
  local copies, waits for them, and re-layouts  2.08 us (4%)
  between operations  0.65 us (1%)
    pallas_call x1, Pallas kernels, shards(): pl.pallas_call(functools.partial(main_kernel, n_grp, n_tile), out_shape=(...  46.9 us
    unnamed x4, local copies, waits for them, and re-layouts  2.08 us

profile of v5, /device:TPU:1, one launch (start us, length us, event | category | flops | bytes accessed | tf_op | source)
XLA Modules:
  0.0 49.7 jit_solution(1966358755217458024)
XLA Ops:
  0.6 46.9 %adjoint.1 = (f32[2,32,512]{2,1,0:T(8,128)}, f32[128]{0:T(128)}) custom-call(f32[2,32,512]{2,1,0:T(8,128)} %vel_h.1, f32[2,32,512]{2,1,0:T(8,128)} %stress_h.1, f32[2,32,512]{2,1,0:T(8,128)} %visc_h.1, f32[32,512]{1,0:T(8,128)} %fric_h.1, s32[32,512]{1,0:T(8,128)} %elem_h.1, f32[512,256]{1,0:T(8,128)} %observed_h.1, f32[2,512,256]{2,1,0:T(8,128)} %look_h.1, ...), custom_call_target="tpu_custom_call" | custom-call | tf_op jit(solution)/shard_map/adjoint/pallas_call | solution.py:514
  47.6 0.0 copy-start
  47.6 1.6 %copy.13 = f32[2,32,512]{2,1,0:T(8,128)} copy(f32[2,32,512]{2,1,0:T(8,128)} %get-tuple-element.4) | data formatting | bytes 262144
  49.1 0.0 copy-done
  49.1 0.5 %copy.14 = f32[128]{0:T(128)} copy(f32[128]{0:T(128)S(1)} %copy-done) | data formatting | bytes 1024
Async XLA Ops:
  47.6 1.6 %copy-start = (f32[128]{0:T(128)S(1)}, f32[128]{0:T(128)}, u32[]{:S(2)}) copy-start(f32[128]{0:T(128)} %get-tuple-element.5) | copy-start | bytes 1540

commit v6 on v5

--- a/solution.py
+++ b/solution.py
@@ -389,14 +389,18 @@
         return jnp.where(lane8 < 64, roll(a, -32), roll(b, 32))
 
     scale = 1.0 / 16.0
+
+    def misfit_adjoint(r, m):
+        u = collect(fields2, W, r, m)
+        v = collect(fields2, EX + W, r, m)
+        rows, at = pl.ds(8 * r, 8), pl.ds(LANES * m, LANES)
+        sxx, sxy, syy, sxo, syo = [gram[pl.ds(j * CX + 8 * r, 8), at] for j in range(5)]
+        adj_n[0, rows, at] = scale * (sxx * u + sxy * v - sxo)
+        adj_n[1, rows, at] = scale * (sxy * u + syy * v - syo)
+
     for r in range(CX // 8):
-        for m in range(CY // LANES):
-            u = collect(fields2, W, r, m)
-            v = collect(fields2, EX + W, r, m)
-            at = pl.ds(LANES * m, LANES)
-            sxx, sxy, syy, sxo, syo = [gram[pl.ds(j * CX + 8 * r, 8), at] for j in range(5)]
-            adj_n[0, pl.ds(8 * r, 8), at] = scale * (sxx * u + sxy * v - sxo)
-            adj_n[1, pl.ds(8 * r, 8), at] = scale * (sxy * u + syy * v - syo)
+        misfit_adjoint(r, 0)
+        misfit_adjoint(r, CY // LANES - 1)
         rows = pl.ds(8 * r, 8)
         aedge_l[rows, :] = jnp.where(
             lane8 < 16, adj_n[0, rows, pl.ds(0, LANES)], roll(adj_n[1, rows, pl.ds(0, LANES)], 16)
@@ -408,7 +412,11 @@
     amoves = neighbours(
         [(rows_of(adj_n), adj_t, adj_b)], aedge_l, aedge_r, ahalo_l, ahalo_r, asend_sem, arecv_sem
     )
-    begin(amoves)
+    begin(amoves[:-2])
+    for r in range(CX // 8):
+        for m in range(1, CY // LANES - 1):
+            misfit_adjoint(r, m)
+    begin(amoves[-2:])
     grads[...] = jnp.zeros_like(grads)
     arrive(amoves)
     adj2 = adj.reshape(2 * EX * SEG, LANES)

time: 49.8 us -> 49.8 us (level)
  no operation moved by 1% of the time
where the time goes in v6:
time: 49.8 us; the launch traced here: 49.7 us
  Pallas kernels  46.9 us (94%)
  local copies, waits for them, and re-layouts  2.08 us (4%)
  between operations  0.65 us (1%)
    pallas_call x1, Pallas kernels, shards(): pl.pallas_call(functools.partial(main_kernel, n_grp, n_tile), out_shape=(...  46.9 us
    unnamed x4, local copies, waits for them, and re-layouts  2.08 us

profile of v6, /device:TPU:1, one launch (start us, length us, event | category | flops | bytes accessed | tf_op | source)
XLA Modules:
  0.0 49.7 jit_solution(2085175298874192598)
XLA Ops:
  0.6 46.9 %adjoint.1 = (f32[2,32,512]{2,1,0:T(8,128)}, f32[128]{0:T(128)}) custom-call(f32[2,32,512]{2,1,0:T(8,128)} %vel_h.1, f32[2,32,512]{2,1,0:T(8,128)} %stress_h.1, f32[2,32,512]{2,1,0:T(8,128)} %visc_h.1, f32[32,512]{1,0:T(8,128)} %fric_h.1, s32[32,512]{1,0:T(8,128)} %elem_h.1, f32[512,256]{1,0:T(8,128)} %observed_h.1, f32[2,512,256]{2,1,0:T(8,128)} %look_h.1, ...), custom_call_target="tpu_custom_call" | custom-call | tf_op jit(solution)/shard_map/adjoint/pallas_call | solution.py:522
  47.6 0.0 copy-start
  47.6 1.6 %copy.13 = f32[2,32,512]{2,1,0:T(8,128)} copy(f32[2,32,512]{2,1,0:T(8,128)} %get-tuple-element.4) | data formatting | bytes 262144
  49.1 0.0 copy-done
  49.1 0.5 %copy.14 = f32[128]{0:T(128)} copy(f32[128]{0:T(128)S(1)} %copy-done) | data formatting | bytes 1024
Async XLA Ops:
  47.6 1.6 %copy-start = (f32[128]{0:T(128)S(1)}, f32[128]{0:T(128)}, u32[]{:S(2)}) copy-start(f32[128]{0:T(128)} %get-tuple-element.5) | copy-start | bytes 1540
